TPU v7x, 32 devices: a whole 2x2x4 slice. The times are simulated.
32 devices in a mesh: wide: 8 (over z, x), narrow: 4 (over y, core).
Axes of the slice: x: 2, y: 2, z: 4, core: 2. Of those that a mesh axis runs over, the one named last changes fastest.
Arguments:
- density: bfloat16 [4096, 4096], P('wide', 'narrow'), may hold values from -0.0059814453 to 0.0059814453
- block_slot: int32 [32], replicated, may hold values from 0 to 31, as said below
- region_blocks: int32 [512], P(('wide', 'narrow')), may hold values from 0 to 31, as said below
- basis_lists: int32 [384, 8], P(('wide', 'narrow')), may hold values from 0 to 15, as said below
- point_counts: int32 [384], P(('wide', 'narrow')), may hold values from 1 to 256
- orbitals: bfloat16 [384, 1024, 256], P(('wide', 'narrow')), may hold values from -6 to 6
- weights: float32 [384, 256], P(('wide', 'narrow')), may hold values from 0.01 to 0.1
- harmonics: bfloat16 [384, 64, 256], P(('wide', 'narrow')), may hold values from -32 to 32
Outputs:
- hamiltonian: float32 [4096, 4096], P('wide', 'narrow')
Inputs may be any that keep to these rules, and one draw needn't show every extreme that they name: `block_slot`: a permutation of the 32 layout slots. `region_blocks`: the 16 blocks of one region are distinct; among the 256 block pairs of one region, no owner of the layout holds more than 8, and some owner holds exactly 8. `basis_lists`: the 8 positions of one list are distinct.
All inputs are finite; a program needn't handle non-finite values.
Results may differ from a plain program's by a relative error of at most 0.0023.
Values may be sent and summed in bfloat16 or wider, within the bound.
A program may use at most 128 MiB of HBM per device.

v0:
```python
import math

import jax
import jax.numpy as jnp
from jax import lax
from jax.sharding import PartitionSpec as P

BLK = 128
PTS = 256
K = 8
S = 16
NL = 64
QB = 4


FAR_COEFF = 10.0


def pair_routes(slots, wide_count, narrow_count):
    width_here = slots.shape[-1]
    lead = slots.shape[:-1]
    row_slot = jnp.broadcast_to(slots[..., :, None], lead + (width_here, width_here)).reshape(
        lead + (width_here * width_here,)
    )
    col_slot = jnp.broadcast_to(slots[..., None, :], lead + (width_here, width_here)).reshape(
        lead + (width_here * width_here,)
    )
    owners = row_slot % wide_count * narrow_count + col_slot % narrow_count
    local_pos = jnp.stack([row_slot // wide_count, col_slot // narrow_count], axis=-1)
    return (owners, local_pos)


def per_device(
    density, block_slot, region_blocks, basis_lists, point_counts, orbitals, weights, harmonics
):
    wide_count = lax.axis_size("wide")
    narrow_count = lax.axis_size("narrow")
    devices_all = wide_count * narrow_count
    capacity = max(1, S // wide_count) * (S // narrow_count)
    slot_count = devices_all * capacity
    batch_count = basis_lists.shape[0]
    col_blocks = density.shape[1] // BLK
    own_slots = block_slot[region_blocks]
    owners, local_pos = pair_routes(own_slots, wide_count, narrow_count)
    hit_table = (owners[:, None] == jnp.arange(devices_all)[None, :]).astype(jnp.int32)
    rank_in = jnp.sum(jnp.cumsum(hit_table, axis=0) * hit_table, axis=1) - 1
    position = owners * capacity + rank_in
    wanted = jnp.zeros((slot_count, 2), jnp.int32).at[position].set(local_pos)
    incoming = lax.all_to_all(wanted, ("wide", "narrow"), split_axis=0, concat_axis=0, tiled=True)
    blocks_four = density.reshape(QB, BLK, col_blocks, BLK)
    outgoing = blocks_four[incoming[:, 0], :, incoming[:, 1], :]
    arrived = lax.all_to_all(outgoing, ("wide", "narrow"), split_axis=0, concat_axis=0, tiled=True)
    region_density = arrived[position].reshape(S, S, BLK, BLK)
    orb_four = orbitals.reshape(batch_count, K, BLK, PTS)

    def batch_density(inner):
        list_row, orb_rows = inner
        sub_matrix = region_density[list_row[:, None], list_row[None, :]]
        product = jnp.einsum(
            "acij,cjp->aip", sub_matrix, orb_rows, preferred_element_type=jnp.float32
        )
        return jnp.sum(product * orb_rows.astype(jnp.float32), axis=(0, 1))

    dens_pts = lax.map(batch_density, (basis_lists, orb_four))
    live_mask = jnp.arange(PTS)[None, :] < point_counts[:, None]
    live_weight = jnp.where(live_mask, weights, jnp.float32(0.0))
    harm_float = harmonics.astype(jnp.float32)
    local_moments = jnp.sum((live_weight * dens_pts)[:, None, :] * harm_float, axis=(0, 2))
    moments = lax.psum(local_moments, ("wide", "narrow"))
    total_points = batch_count * PTS * devices_all
    far_field = (
        FAR_COEFF
        * jnp.sum(moments[None, :, None] * harm_float, axis=1)
        / math.sqrt(total_points * NL)
    )
    potential = 0.5 * dens_pts - (1.0 + dens_pts * dens_pts) ** (1.0 / 6.0) + far_field
    factor = live_weight * potential
    scaled = (orb_four.astype(jnp.float32) * factor[:, None, None, :]).astype(jnp.bfloat16)

    def add_batch(partial_h, inner):
        list_row, scaled_rows, orb_rows = inner
        term = jnp.einsum(
            "aip,cjp->acij", scaled_rows, orb_rows, preferred_element_type=jnp.float32
        )
        return (partial_h.at[list_row[:, None], list_row[None, :]].add(term), None)

    start = jnp.zeros((S, S, BLK, BLK), jnp.float32)
    partial_h = lax.scan(add_batch, start, (basis_lists, scaled, orb_four))[0]
    send_back = (
        jnp.zeros((slot_count, BLK, BLK), jnp.bfloat16)
        .at[position]
        .set(partial_h.reshape(S * S, BLK, BLK).astype(jnp.bfloat16))
    )
    returned = lax.all_to_all(
        send_back, ("wide", "narrow"), split_axis=0, concat_axis=0, tiled=True
    )
    accum = jnp.zeros((QB, BLK, col_blocks, BLK), jnp.float32)
    accum = accum.at[incoming[:, 0], :, incoming[:, 1], :].add(returned.astype(jnp.float32))
    return accum.reshape(density.shape)


def solution(mesh):
    in_specs = (
        P("wide", "narrow"),
        P(),
        P(("wide", "narrow")),
        P(("wide", "narrow"), None),
        P(("wide", "narrow")),
        P(("wide", "narrow"), None, None),
        P(("wide", "narrow"), None),
        P(("wide", "narrow"), None, None),
    )
    out_specs = P("wide", "narrow")
    return jax.shard_map(
        per_device, mesh=mesh, in_specs=in_specs, out_specs=out_specs, check_vma=False
    )
```

profile of v0, /device:TPU:0, one launch (start us, length us, event | category | flops | bytes accessed | tf_op | source)
XLA Modules:
  0.0 940.8 jit_solution(15712613102842991055)
XLA Ops:
  5.3 7.3 all-to-all-start
  14.4 5.5 all-to-all-done
  20.0 10.0 %gather_fusion.2 = bf16[256,128,128]{2,1,0:T(8,128)(2,1)} fusion(bf16[4,128,8,128]{3,1,2,0:T(8,128)(2,1)S(1)} %copy.30, s32[256]{0:T(256)S(1)} %bitcast.116), kind=kCustom, calls=%fused_computation.2 | custom fusion | bytes 16779264 | tf_op jit(solution)/shard_map/gather | solution.py:51
  34.0 185.2 %all-to-all-done.1 = bf16[256,128,128]{2,1,0:T(8,128)(2,1)} async-done(((bf16[256,128,128]{2,1,0:T(8,128)(2,1)}), bf16[256,128,128]{2,1,0:T(8,128)(2,1)}, u32[]{:S(2)}, u32[]{:S(2)}) %all-to-all-start.1) | async-done | bytes 8388640 | tf_op jit(solution)/shard_map/all_to_all | solution.py:52
  219.1 12.0 %gather_fusion.3 = bf16[256,128,128]{2,1,0:T(8,128)(2,1)} fusion(bf16[256,128,128]{2,1,0:T(8,128)(2,1)} %all-to-all-done.1, s32[1024]{0:T(1024)S(1)} %pad_clamp_fusion), kind=kCustom, calls=%fused_computation.3 | custom fusion | bytes 16778240 | tf_op jit(solution)/shard_map/gather | solution.py:53
  231.1 78.8 %while.22 = (s32[]{:T(128)}, f32[12,256]{1,0:T(8,128)S(1)}, s32[12,8]{1,0:T(8,128)S(1)}, bf16[16,16,128,128]{3,2,1,0:T(8,128)(2,1)}, bf16[12,8,128,256]{3,2,1,0:T(8,128)(2,1)}) while((s32[]{:T(128)}, f32[12,256]{1,0:T(8,128)S(1)}, s32[12,8]{1,0:T(8,128)S(1)}, bf16[16,16,128,128]{3,2,1,0:T(8,128)(2,1)}, ...), condition=%wide.region_6.7_spmd.clone, body=%wide.region_4.6_spmd.sunk.clone | while | flops 537657216 | bytes 7345673 | solution.py:64
  231.3 4.3 gather_fusion
  237.9 4.3 gather_fusion
  244.4 4.3 gather_fusion
  251.0 4.3 gather_fusion
  264.1 4.3 gather_fusion
  277.2 4.3 gather_fusion
  290.4 4.3 gather_fusion
  297.0 4.3 gather_fusion
  310.2 41.5 %psum.7 = f32[64]{0:T(128)S(1)} all-reduce(f32[64]{0:T(128)S(1)} %fusion.16), channel_id=1, replica_groups=mesh['wide'=8,'narrow'=4] {'wide','narrow'}, use_global_device_ids=true, to_apply=%region_8.9 | all-reduce | flops 64 | bytes 512 | tf_op jit(solution)/shard_map/psum | solution.py:69
  352.0 7.4 multiply_convert_fusion
  359.4 7.8 broadcast_in_dim.112
  367.3 283.8 %while.23 = (s32[]{:T(128)}, f32[16,16,128,128]{3,2,1,0:T(8,128)}, s32[12,8]{1,0:T(8,128)S(1)}, bf16[12,8,128,256]{3,2,1,0:T(8,128)(2,1)}, bf16[12,8,128,256]{3,2,1,0:T(8,128)(2,1)}) while((s32[]{:T(128)}, f32[16,16,128,128]{3,2,1,0:T(8,128)}, s32[12,8]{1,0:T(8,128)S(1)}, bf16[12,8,128,256]{3,2,1,0:T(8,128)(2,1)}, ...), condition=%wide.region_12.13_spmd.clone, body=%wide.region_10.12_spmd.sunk.clone | while | flops 537919808 | bytes 26217088 | solution.py:88
  371.5 5.3 copy.46
  376.8 14.1 %scatter_fusion = f32[16,16,128,128]{3,2,1,0:T(8,128)} fusion(f32[16,16,128,128]{3,2,1,0:T(8,128)} %get-tuple-element.260, s32[64]{0:T(128)S(1)} %reshape.464, f32[64,128,128]{2,1,0:T(8,128)} %bitcast.111), kind=kCustom, calls=%fused_computation.4.clone.1.clone | custom fusion | flops 1048576 | bytes 12583424 | tf_op jit(solution)/shard_map/while/body/eval_jaxpr/scatter-add | solution.py:85
  395.1 5.3 copy.46
  400.5 14.1 %scatter_fusion = f32[16,16,128,128]{3,2,1,0:T(8,128)} fusion(f32[16,16,128,128]{3,2,1,0:T(8,128)} %get-tuple-element.260, s32[64]{0:T(128)S(1)} %reshape.464, f32[64,128,128]{2,1,0:T(8,128)} %bitcast.111), kind=kCustom, calls=%fused_computation.4.clone.1.clone | custom fusion | flops 1048576 | bytes 12583424 | tf_op jit(solution)/shard_map/while/body/eval_jaxpr/scatter-add | solution.py:85
  418.8 5.3 copy.46
  424.1 14.1 %scatter_fusion = f32[16,16,128,128]{3,2,1,0:T(8,128)} fusion(f32[16,16,128,128]{3,2,1,0:T(8,128)} %get-tuple-element.260, s32[64]{0:T(128)S(1)} %reshape.464, f32[64,128,128]{2,1,0:T(8,128)} %bitcast.111), kind=kCustom, calls=%fused_computation.4.clone.1.clone | custom fusion | flops 1048576 | bytes 12583424 | tf_op jit(solution)/shard_map/while/body/eval_jaxpr/scatter-add | solution.py:85
  442.4 5.3 copy.46
  447.7 14.0 %scatter_fusion = f32[16,16,128,128]{3,2,1,0:T(8,128)} fusion(f32[16,16,128,128]{3,2,1,0:T(8,128)} %get-tuple-element.260, s32[64]{0:T(128)S(1)} %reshape.464, f32[64,128,128]{2,1,0:T(8,128)} %bitcast.111), kind=kCustom, calls=%fused_computation.4.clone.1.clone | custom fusion | flops 1048576 | bytes 12583424 | tf_op jit(solution)/shard_map/while/body/eval_jaxpr/scatter-add | solution.py:85
  465.9 5.3 copy.46
  471.3 14.2 %scatter_fusion = f32[16,16,128,128]{3,2,1,0:T(8,128)} fusion(f32[16,16,128,128]{3,2,1,0:T(8,128)} %get-tuple-element.260, s32[64]{0:T(128)S(1)} %reshape.464, f32[64,128,128]{2,1,0:T(8,128)} %bitcast.111), kind=kCustom, calls=%fused_computation.4.clone.1.clone | custom fusion | flops 1048576 | bytes 12583424 | tf_op jit(solution)/shard_map/while/body/eval_jaxpr/scatter-add | solution.py:85
  489.7 5.3 copy.46
  495.1 14.2 %scatter_fusion = f32[16,16,128,128]{3,2,1,0:T(8,128)} fusion(f32[16,16,128,128]{3,2,1,0:T(8,128)} %get-tuple-element.260, s32[64]{0:T(128)S(1)} %reshape.464, f32[64,128,128]{2,1,0:T(8,128)} %bitcast.111), kind=kCustom, calls=%fused_computation.4.clone.1.clone | custom fusion | flops 1048576 | bytes 12583424 | tf_op jit(solution)/shard_map/while/body/eval_jaxpr/scatter-add | solution.py:85
  513.5 5.3 copy.46
  518.8 14.1 %scatter_fusion = f32[16,16,128,128]{3,2,1,0:T(8,128)} fusion(f32[16,16,128,128]{3,2,1,0:T(8,128)} %get-tuple-element.260, s32[64]{0:T(128)S(1)} %reshape.464, f32[64,128,128]{2,1,0:T(8,128)} %bitcast.111), kind=kCustom, calls=%fused_computation.4.clone.1.clone | custom fusion | flops 1048576 | bytes 12583424 | tf_op jit(solution)/shard_map/while/body/eval_jaxpr/scatter-add | solution.py:85
  537.1 5.3 copy.46
  542.5 14.1 %scatter_fusion = f32[16,16,128,128]{3,2,1,0:T(8,128)} fusion(f32[16,16,128,128]{3,2,1,0:T(8,128)} %get-tuple-element.260, s32[64]{0:T(128)S(1)} %reshape.464, f32[64,128,128]{2,1,0:T(8,128)} %bitcast.111), kind=kCustom, calls=%fused_computation.4.clone.1.clone | custom fusion | flops 1048576 | bytes 12583424 | tf_op jit(solution)/shard_map/while/body/eval_jaxpr/scatter-add | solution.py:85
  560.7 5.3 copy.46
  566.1 14.1 %scatter_fusion = f32[16,16,128,128]{3,2,1,0:T(8,128)} fusion(f32[16,16,128,128]{3,2,1,0:T(8,128)} %get-tuple-element.260, s32[64]{0:T(128)S(1)} %reshape.464, f32[64,128,128]{2,1,0:T(8,128)} %bitcast.111), kind=kCustom, calls=%fused_computation.4.clone.1.clone | custom fusion | flops 1048576 | bytes 12583424 | tf_op jit(solution)/shard_map/while/body/eval_jaxpr/scatter-add | solution.py:85
  584.4 5.3 copy.46
  589.7 14.1 %scatter_fusion = f32[16,16,128,128]{3,2,1,0:T(8,128)} fusion(f32[16,16,128,128]{3,2,1,0:T(8,128)} %get-tuple-element.260, s32[64]{0:T(128)S(1)} %reshape.464, f32[64,128,128]{2,1,0:T(8,128)} %bitcast.111), kind=kCustom, calls=%fused_computation.4.clone.1.clone | custom fusion | flops 1048576 | bytes 12583424 | tf_op jit(solution)/shard_map/while/body/eval_jaxpr/scatter-add | solution.py:85
  608.0 5.3 copy.46
  613.4 14.0 %scatter_fusion = f32[16,16,128,128]{3,2,1,0:T(8,128)} fusion(f32[16,16,128,128]{3,2,1,0:T(8,128)} %get-tuple-element.260, s32[64]{0:T(128)S(1)} %reshape.464, f32[64,128,128]{2,1,0:T(8,128)} %bitcast.111), kind=kCustom, calls=%fused_computation.4.clone.1.clone | custom fusion | flops 1048576 | bytes 12583424 | tf_op jit(solution)/shard_map/while/body/eval_jaxpr/scatter-add | solution.py:85
  631.6 5.3 copy.46
  637.0 14.1 %scatter_fusion = f32[16,16,128,128]{3,2,1,0:T(8,128)} fusion(f32[16,16,128,128]{3,2,1,0:T(8,128)} %get-tuple-element.260, s32[64]{0:T(128)S(1)} %reshape.464, f32[64,128,128]{2,1,0:T(8,128)} %bitcast.111), kind=kCustom, calls=%fused_computation.4.clone.1.clone | custom fusion | flops 1048576 | bytes 12583424 | tf_op jit(solution)/shard_map/while/body/eval_jaxpr/scatter-add | solution.py:85
  651.1 9.2 convert_element_type.30
  660.3 5.3 broadcast_in_dim.111
  665.6 37.3 %scatter_fusion.1 = bf16[256,128,128]{2,1,0:T(8,128)(2,1)} fusion(bf16[256,128,128]{2,1,0:T(8,128)(2,1)} %broadcast_in_dim.111, s32[256]{0:T(256)S(1)} %bitcast.125, bf16[256,128,128]{2,1,0:T(8,128)(2,1)} %bitcast.114), kind=kCustom, calls=%fused_computation.6 | custom fusion | bytes 25166848 | tf_op jit(solution)/shard_map/scatter | solution.py:92
  702.9 188.7 %all_to_all.22 = bf16[256,128,128]{2,1,0:T(8,128)(2,1)} all-to-all(bf16[256,128,128]{2,1,0:T(8,128)(2,1)} %scatter_fusion.1), channel_id=1, replica_groups=mesh['wide'=8,'narrow'=4] {'wide','narrow'}, dimensions={0} | all-to-all | bytes 16777216 | tf_op jit(solution)/shard_map/all_to_all | solution.py:94
  891.6 11.2 %convert_element_type.32 = f32[256,128,128]{2,1,0:T(8,128)} convert(bf16[256,128,128]{2,1,0:T(8,128)(2,1)} %all_to_all.22) | non-fusion elementwise | flops 4194304 | bytes 25165824 | tf_op jit(solution)/shard_map/convert_element_type | solution.py:98
  903.1 34.7 %scatter_fusion.2 = f32[4,128,8,128]{3,1,2,0:T(8,128)S(1)} fusion(f32[4,128,8,128]{3,1,2,0:T(8,128)S(1)} %broadcast_in_dim.98, s32[256]{0:T(256)S(1)} %bitcast.115, f32[256,128,128]{2,1,0:T(8,128)} %convert_element_type.32), kind=kCustom, calls=%fused_computation.7 | custom fusion | flops 4194304 | bytes 50333696 | tf_op jit(solution)/shard_map/scatter-add | solution.py:98
  (194 shorter events, 108.6 us)
Async XLA Ops:
  0.0 0.7 copy-start
  5.3 14.6 %all-to-all-start = ((s32[32,8,2]{1,2,0:T(2,128)}), s32[32,8,2]{1,2,0:T(2,128)S(1)}, u32[]{:S(2)}, u32[]{:S(2)}) async-start(s32[32,8,2]{1,2,0:T(2,128)} %copy.28), calls=%async_computation | async-start | bytes 65536 | tf_op jit(solution)/shard_map/all_to_all | solution.py:49
  30.0 3.8 copy-start.4
  30.0 189.1 %all-to-all-start.1 = ((bf16[256,128,128]{2,1,0:T(8,128)(2,1)}), bf16[256,128,128]{2,1,0:T(8,128)(2,1)}, u32[]{:S(2)}, u32[]{:S(2)}) async-start(bf16[256,128,128]{2,1,0:T(8,128)(2,1)} %gather_fusion.2), calls=%async_computation.1 | async-start | bytes 16777216 | tf_op jit(solution)/shard_map/all_to_all | solution.py:52
  231.1 78.8 %copy-start.3 = (f32[12,256]{1,0:T(8,128)S(1)}, f32[12,256]{1,0:T(8,128)}, u32[]{:S(2)}) copy-start(f32[12,256]{1,0:T(8,128)} %param.18) | copy-start | bytes 36868
  231.1 78.8 %copy-start.5 = (s32[12]{0:T(128)S(1)}, s32[12]{0:T(128)}, u32[]{:S(2)}) copy-start(s32[12]{0:T(128)} %param.16) | copy-start | bytes 148
  231.1 78.9 %copy-start.2 = (bf16[12,64,256]{2,1,0:T(8,128)(2,1)S(1)}, bf16[12,64,256]{2,1,0:T(8,128)(2,1)}, u32[]{:S(2)}) copy-start(bf16[12,64,256]{2,1,0:T(8,128)(2,1)} %param.19) | copy-start | bytes 1179652
  903.1 37.8 %copy-start.1 = (s32[32]{0:T(128)S(1)}, s32[32]{0:T(128)}, u32[]{:S(2)}) copy-start(s32[32]{0:T(128)} %param.13) | copy-start | bytes 388
where the time goes:
time: 946 us; the launch traced here: 941 us
  other arithmetic  236 us (25%)
  blocking collectives  230 us (24%)
  local copies, waits for them, and re-layouts  200 us (21%)
  waiting for transfers between devices  191 us (20%)
  matrix products  71.7 us (8%)
  starting transfers between devices  11.1 us (1%)
    all_to_all x1, blocking collectives, per_device(): lax.all_to_all(send_back, ('wide', 'narrow'), split_axis=0, concat_axis=0...  189 us
    all_to_all x1, waiting for transfers between devices, per_device(): lax.all_to_all(outgoing, ('wide', 'narrow'), split_axis=0, concat_axis=0,...  185 us
    scatter-add x12, other arithmetic, add_batch(): return (partial_h.at[list_row[:, None], list_row[None, :]].add(term), None)  169 us
    transpose x12, local copies, waits for them, and re-layouts, add_batch(): jnp.einsum('aip,cjp->acij', scaled_rows, orb_rows, preferred_element_type...  64.1 us
    gather x12, local copies, waits for them, and re-layouts, batch_density(): sub_matrix = region_density[list_row[:, None], list_row[None, :]]  52.1 us
    dot_general x12, matrix products, add_batch(): jnp.einsum('aip,cjp->acij', scaled_rows, orb_rows, preferred_element_type...  48.3 us
    psum x1, blocking collectives, per_device(): moments = lax.psum(local_moments, ('wide', 'narrow'))  41.5 us
    scatter x1, local copies, waits for them, and re-layouts, per_device(): send_back = jnp.zeros((slot_count, BLK, BLK), jnp.bfloat16).at[position]....  37.3 us
  transfers between devices with their start and end apart: 2, of which 2 were waited for; matrix products, arithmetic and copies ran while one was open for 0% of the time, Pallas kernels for 0%

commit v1 on v0

v1 whole, which is shorter than its diff:
```python
import functools
import math

import jax
import jax.numpy as jnp
from jax import lax
from jax.experimental import pallas as pl
from jax.experimental.pallas import tpu as pltpu
from jax.sharding import PartitionSpec as P

BLK = 128
FAR_COEFF = 10.0
RING = 4
LANES = 128
MESH = pl.DeviceIdType.MESH
VMEM_BYTES = 58 * 1024 * 1024


def plane_peer(offset, inner, narrow):
    wide_me = lax.axis_index("wide")
    group = inner * narrow
    base = wide_me // inner * inner
    mine = wide_me % inner * narrow + lax.axis_index("narrow")
    other = lax.rem(mine + offset, group)
    return mine, other, (base + other // narrow, other % narrow)


def plane_barrier(inner, narrow):
    barrier = pltpu.get_barrier_semaphore()
    for offset in range(1, inner * narrow):
        _, _, device = plane_peer(offset, inner, narrow)
        pl.semaphore_signal(barrier, inc=1, device_id=device, device_id_type=MESH)
    pl.semaphore_wait(barrier, inner * narrow - 1)


def tile_kernel(inner, narrow, tile_ref, out_ref, send_sem, recv_sem):
    plane_barrier(inner, narrow)
    copies = []
    for offset in range(1, inner * narrow):
        mine, _, device = plane_peer(offset, inner, narrow)
        copy = pltpu.make_async_remote_copy(
            src_ref=tile_ref,
            dst_ref=out_ref.at[mine],
            send_sem=send_sem.at[offset - 1],
            recv_sem=recv_sem.at[offset - 1],
            device_id=device,
            device_id_type=MESH,
        )
        copy.start()
        copies.append(copy)
    mine, _, _ = plane_peer(0, inner, narrow)
    out_ref[mine] = tile_ref[...]
    for copy in copies:
        copy.wait()


def share_tile(tile, inner, narrow):
    group = inner * narrow
    return pl.pallas_call(
        functools.partial(tile_kernel, inner, narrow),
        out_shape=jax.ShapeDtypeStruct((group,) + tile.shape, tile.dtype),
        in_specs=[pl.BlockSpec(memory_space=pltpu.VMEM)],
        out_specs=pl.BlockSpec(memory_space=pltpu.VMEM),
        scratch_shapes=[
            pltpu.SemaphoreType.DMA((group - 1,)),
            pltpu.SemaphoreType.DMA((group - 1,)),
        ],
        compiler_params=pltpu.CompilerParams(collective_id=0, has_side_effects=True),
        name="share_tile",
    )(tile)


def exchange_kernel(inner, narrow, src_ref, out_ref, own, send_sem, recv_sem, own_sem):
    mine, _, _ = plane_peer(0, inner, narrow)
    take = pltpu.make_async_copy(src_ref.at[mine], own, own_sem.at[0])
    take.start()
    plane_barrier(inner, narrow)
    copies = []
    for offset in range(1, inner * narrow):
        _, other, device = plane_peer(offset, inner, narrow)
        copy = pltpu.make_async_remote_copy(
            src_ref=src_ref.at[other],
            dst_ref=out_ref.at[mine],
            send_sem=send_sem.at[offset - 1],
            recv_sem=recv_sem.at[offset - 1],
            device_id=device,
            device_id_type=MESH,
        )
        copy.start()
        copies.append(copy)
    take.wait()
    put = pltpu.make_async_copy(own, out_ref.at[mine], own_sem.at[1])
    put.start()
    put.wait()
    for copy in copies:
        copy.wait()


def exchange(blocks, inner, narrow):
    group = inner * narrow
    size = math.prod(blocks.shape) * 2
    return pl.pallas_call(
        functools.partial(exchange_kernel, inner, narrow),
        out_shape=jax.ShapeDtypeStruct(blocks.shape, blocks.dtype),
        in_specs=[pl.BlockSpec(memory_space=pl.ANY)],
        out_specs=pl.BlockSpec(memory_space=pl.ANY),
        scratch_shapes=[
            pltpu.VMEM(blocks.shape[1:], blocks.dtype),
            pltpu.SemaphoreType.DMA((group - 1,)),
            pltpu.SemaphoreType.DMA((group - 1,)),
            pltpu.SemaphoreType.DMA((2,)),
        ],
        compiler_params=pltpu.CompilerParams(collective_id=1, has_side_effects=True),
        cost_estimate=pl.CostEstimate(
            flops=0, bytes_accessed=size * 32, transcendentals=0
        ),
        name="exchange",
    )(blocks)


def total_kernel(devices, narrow, tile_ref, out_ref, held, send_sem, recv_sem):
    mine = lax.axis_index("wide") * narrow + lax.axis_index("narrow")

    def device_at(offset):
        other = lax.rem(mine + offset, devices)
        return (other // narrow, other % narrow)

    barrier = pltpu.get_barrier_semaphore()

    def greet(offset, carry):
        pl.semaphore_signal(
            barrier, inc=1, device_id=device_at(offset), device_id_type=MESH
        )
        return carry

    def copy_at(offset):
        return pltpu.make_async_remote_copy(
            src_ref=tile_ref,
            dst_ref=held.at[mine],
            send_sem=send_sem.at[offset - 1],
            recv_sem=recv_sem.at[offset - 1],
            device_id=device_at(offset),
            device_id_type=MESH,
        )

    def send(offset, carry):
        copy_at(offset).start()
        return carry

    def finish(offset, carry):
        copy_at(offset).wait()
        return carry

    lax.fori_loop(1, devices, greet, 0)
    pl.semaphore_wait(barrier, devices - 1)
    lax.fori_loop(1, devices, send, 0)
    held[mine] = tile_ref[...]
    lax.fori_loop(1, devices, finish, 0)
    out_ref[...] = jnp.sum(held[...], axis=0)


def total_over_devices(tile, devices, narrow):
    return pl.pallas_call(
        functools.partial(total_kernel, devices, narrow),
        out_shape=jax.ShapeDtypeStruct(tile.shape, tile.dtype),
        in_specs=[pl.BlockSpec(memory_space=pltpu.VMEM)],
        out_specs=pl.BlockSpec(memory_space=pltpu.VMEM),
        scratch_shapes=[
            pltpu.VMEM((devices,) + tile.shape, tile.dtype),
            pltpu.SemaphoreType.DMA((devices - 1,)),
            pltpu.SemaphoreType.DMA((devices - 1,)),
        ],
        compiler_params=pltpu.CompilerParams(collective_id=2, has_side_effects=True),
        name="total_over_devices",
    )(tile)


def select_kernel(row_cap, col_cap, rows_ref, cols_ref, dens_ref, out_ref):
    dest = pl.program_id(0)
    for rr in range(row_cap):
        row = pl.multiple_of(rows_ref[dest, rr] * BLK, BLK)
        for cr in range(col_cap):
            col = pl.multiple_of(cols_ref[dest, cr] * BLK, BLK)
            out_ref[0, rr * col_cap + cr] = dens_ref[pl.ds(row, BLK), pl.ds(col, BLK)]


def select(dens, rows, cols):
    group, row_cap = rows.shape
    col_cap = cols.shape[1]
    cap = row_cap * col_cap
    return pl.pallas_call(
        functools.partial(select_kernel, row_cap, col_cap),
        out_shape=jax.ShapeDtypeStruct((group, cap, BLK, BLK), dens.dtype),
        grid_spec=pltpu.PrefetchScalarGridSpec(
            num_scalar_prefetch=2,
            grid=(group,),
            in_specs=[pl.BlockSpec(dens.shape, lambda g, *_: (0, 0))],
            out_specs=pl.BlockSpec((1, cap, BLK, BLK), lambda g, *_: (g, 0, 0, 0)),
        ),
        compiler_params=pltpu.CompilerParams(vmem_limit_bytes=VMEM_BYTES),
        name="select",
    )(rows, cols, dens)


def combine_kernel(row_cap, col_cap, has_prev, rows_ref, cols_ref, got_ref, *rest):
    if has_prev:
        prev_ref, out_ref, acc = rest
    else:
        prev_ref, (out_ref, acc) = None, rest
    source = pl.program_id(0)

    @pl.when(source == 0)
    def _():
        if has_prev:
            acc[...] = prev_ref[...].astype(jnp.float32)
        else:
            acc[...] = jnp.zeros_like(acc)

    for rr in range(row_cap):
        row = pl.multiple_of(rows_ref[source, rr] * BLK, BLK)
        for cr in range(col_cap):
            col = pl.multiple_of(cols_ref[source, cr] * BLK, BLK)
            acc[pl.ds(row, BLK), pl.ds(col, BLK)] += got_ref[
                0, rr * col_cap + cr
            ].astype(jnp.float32)

    @pl.when(source == pl.num_programs(0) - 1)
    def _():
        out_ref[...] = acc[...].astype(out_ref.dtype)


def combine(got, prev, rows, cols, shape, dtype):
    group, row_cap = rows.shape
    col_cap = cols.shape[1]
    cap = row_cap * col_cap
    whole = pl.BlockSpec(shape, lambda g, *_: (0, 0))
    specs = [pl.BlockSpec((1, cap, BLK, BLK), lambda g, *_: (g, 0, 0, 0))]
    operands = [got]
    if prev is not None:
        specs.append(whole)
        operands.append(prev)
    return pl.pallas_call(
        functools.partial(combine_kernel, row_cap, col_cap, prev is not None),
        out_shape=jax.ShapeDtypeStruct(shape, dtype),
        grid_spec=pltpu.PrefetchScalarGridSpec(
            num_scalar_prefetch=2,
            grid=(group,),
            in_specs=specs,
            out_specs=whole,
            scratch_shapes=[pltpu.VMEM(shape, jnp.float32)],
        ),
        compiler_params=pltpu.CompilerParams(vmem_limit_bytes=VMEM_BYTES),
        name="combine",
    )(rows, cols, *operands)


def live_row(weights_ref, counts_ref, batch):
    points = weights_ref.shape[1]
    point = lax.broadcasted_iota(jnp.int32, (1, points), 1)
    return jnp.where(
        point < counts_ref[batch], weights_ref[pl.ds(batch, 1), :], jnp.float32(0.0)
    )


def density_kernel(
    steps, list_len, lists_ref, row_ref, col_ref, counts_ref, orb_ref, harm_ref, weights_ref, *rest
):
    chunks = rest[:steps]
    rho_ref, moment_ref, held, matrix, sems = rest[steps:]
    batch = pl.program_id(0)
    per_chunk = held.shape[0] // steps

    @pl.when(batch == 0)
    def _():
        copies = [
            pltpu.make_async_copy(
                chunks[k], held.at[pl.ds(k * per_chunk, per_chunk)], sems.at[k]
            )
            for k in range(steps)
        ]
        for copy in copies:
            copy.start()
        moment_ref[...] = jnp.zeros_like(moment_ref)
        for copy in copies:
            copy.wait()

    places = [lists_ref[batch, k] for k in range(list_len)]
    cols = [col_ref[place] for place in places]
    for k in range(list_len):
        row = row_ref[places[k]]
        for k2 in range(list_len):
            matrix[k * BLK : (k + 1) * BLK, k2 * BLK : (k2 + 1) * BLK] = held[row + cols[k2]]
    orbs = orb_ref[0]
    rows_each = 2 * BLK
    total = jnp.zeros((1, orbs.shape[1]), jnp.float32)
    for top in range(0, list_len * BLK, rows_each):
        product = jnp.dot(
            matrix[top : top + rows_each, :], orbs, preferred_element_type=jnp.float32
        )
        part = product * orb_ref[0, top : top + rows_each, :].astype(jnp.float32)
        total += jnp.sum(part, axis=0, keepdims=True)
    rho_ref[pl.ds(batch, 1), :] = total
    live = live_row(weights_ref, counts_ref, batch) * total
    moment_ref[...] += harm_ref[0].astype(jnp.float32) * live


def density_points(lists, rows, cols, counts, orbitals, harmonics, weights, chunks):
    batches, height, points = orbitals.shape
    list_len = lists.shape[1]
    components = harmonics.shape[1]
    steps = len(chunks)
    blocks = [chunk.reshape(-1, BLK, BLK) for chunk in chunks]
    held = steps * blocks[0].shape[0]
    full = lambda shape: pl.BlockSpec(shape, lambda g, *_: (0, 0))
    return pl.pallas_call(
        functools.partial(density_kernel, steps, list_len),
        out_shape=[
            jax.ShapeDtypeStruct((batches, points), jnp.float32),
            jax.ShapeDtypeStruct((components, points), jnp.float32),
        ],
        grid_spec=pltpu.PrefetchScalarGridSpec(
            num_scalar_prefetch=4,
            grid=(batches,),
            in_specs=[
                pl.BlockSpec((1, height, points), lambda g, *_: (g, 0, 0)),
                pl.BlockSpec((1, components, points), lambda g, *_: (g, 0, 0)),
                full((batches, points)),
            ]
            + [pl.BlockSpec(memory_space=pl.ANY)] * steps,
            out_specs=[full((batches, points)), full((components, points))],
            scratch_shapes=[
                pltpu.VMEM((held, BLK, BLK), jnp.bfloat16),
                pltpu.VMEM((height, height), jnp.bfloat16),
                pltpu.SemaphoreType.DMA((steps,)),
            ],
        ),
        compiler_params=pltpu.CompilerParams(vmem_limit_bytes=VMEM_BYTES),
        name="density_points",
    )(lists, rows, cols, counts, orbitals, harmonics, weights, *blocks)


def integral_kernel(
    steps,
    list_len,
    far_scale,
    lists_ref,
    row_ref,
    col_ref,
    counts_ref,
    orb_ref,
    harm_ref,
    weights_ref,
    rho_ref,
    moment_ref,
    *rest,
):
    outs = rest[:steps]
    acc, stage, sems = rest[steps:]
    batch = pl.program_id(0)
    per_chunk = acc.shape[0] // steps

    @pl.when(batch == 0)
    def _():
        @pl.loop(0, acc.shape[0])
        def _(place):
            acc[place] = jnp.zeros(acc.shape[1:], jnp.float32)

    rho = rho_ref[pl.ds(batch, 1), :]
    far = FAR_COEFF * jnp.sum(
        moment_ref[...] * harm_ref[0].astype(jnp.float32), axis=0, keepdims=True
    )
    sixth = jnp.exp(jnp.log(1.0 + rho * rho) * (1.0 / 6.0))
    potential = 0.5 * rho - sixth + far / far_scale
    factor = live_row(weights_ref, counts_ref, batch) * potential
    orbs = orb_ref[0]
    scaled = (orbs.astype(jnp.float32) * factor).astype(jnp.bfloat16)
    places = [lists_ref[batch, k] for k in range(list_len)]
    rows = [row_ref[place] for place in places]
    cols = [col_ref[place] for place in places]
    for pair in range(0, list_len, 2):
        right = orb_ref[0, pair * BLK : (pair + 2) * BLK, :]
        term = lax.dot_general(
            scaled, right, (((1,), (1,)), ((), ())), preferred_element_type=jnp.float32
        )
        for k in range(list_len):
            for k2 in range(2):
                acc[rows[k] + cols[pair + k2]] += term[
                    k * BLK : (k + 1) * BLK, k2 * BLK : (k2 + 1) * BLK
                ]

    @pl.when(batch == pl.num_programs(0) - 1)
    def _():
        copies = []
        for k in range(steps):
            if k >= 2:
                copies[k - 2].wait()

            @pl.loop(0, per_chunk)
            def _(place, k=k):
                stage[k % 2, place] = acc[k * per_chunk + place].astype(jnp.bfloat16)

            copy = pltpu.make_async_copy(stage.at[k % 2], outs[k], sems.at[k])
            copy.start()
            copies.append(copy)
        for copy in copies[-2:]:
            copy.wait()


def integrals(lists, rows, cols, counts, orbitals, harmonics, weights, rho, moments, steps, held, far_scale):
    batches, height, points = orbitals.shape
    list_len = lists.shape[1]
    components = harmonics.shape[1]
    per_chunk = held // steps
    full = lambda shape: pl.BlockSpec(shape, lambda g, *_: (0, 0))
    return pl.pallas_call(
        functools.partial(integral_kernel, steps, list_len, far_scale),
        out_shape=[jax.ShapeDtypeStruct((per_chunk, BLK, BLK), jnp.bfloat16)] * steps,
        grid_spec=pltpu.PrefetchScalarGridSpec(
            num_scalar_prefetch=4,
            grid=(batches,),
            in_specs=[
                pl.BlockSpec((1, height, points), lambda g, *_: (g, 0, 0)),
                pl.BlockSpec((1, components, points), lambda g, *_: (g, 0, 0)),
                full((batches, points)),
                full((batches, points)),
                full((components, 1)),
            ],
            out_specs=[pl.BlockSpec(memory_space=pl.ANY)] * steps,
            scratch_shapes=[
                pltpu.VMEM((held, BLK, BLK), jnp.float32),
                pltpu.VMEM((2, per_chunk, BLK, BLK), jnp.bfloat16),
                pltpu.SemaphoreType.DMA((steps,)),
            ],
        ),
        compiler_params=pltpu.CompilerParams(vmem_limit_bytes=VMEM_BYTES),
        name="integrals",
    )(lists, rows, cols, counts, orbitals, harmonics, weights, rho, moments)


def rank_among(keys):
    count = keys.shape[0]
    order = jnp.arange(count)
    same = (keys[:, None] == keys[None, :]) & (order[None, :] < order[:, None])
    return jnp.sum(same.astype(jnp.int32), axis=1)


def spread(positions, values, size):
    hit = positions[None, :] == jnp.arange(size)[:, None]
    return jnp.sum(jnp.where(hit, values[None, :], 0), axis=1)


def per_device(
    region, density, block_slot, region_blocks, basis_lists, point_counts, orbitals, weights, harmonics
):
    wide = lax.axis_size("wide")
    narrow = lax.axis_size("narrow")
    devices = wide * narrow
    steps = math.gcd(wide, RING)
    inner = wide // steps
    group = inner * narrow
    row_cap = max(1, region // wide)
    col_cap = region // narrow
    cap = row_cap * col_cap
    wide_me = lax.axis_index("wide")
    narrow_me = lax.axis_index("narrow")
    ring_me = wide_me // inner
    inner_me = wide_me % inner

    known = block_slot.shape[0]
    hit = region_blocks[:, None] == jnp.arange(known)[None, :]
    slots = jnp.sum(jnp.where(hit, block_slot[None, :], 0), axis=1)
    row_owner, row_local = slots % wide, slots // wide
    col_owner, col_local = slots % narrow, slots // narrow
    row_rank, col_rank = rank_among(row_owner), rank_among(col_owner)
    row_table = spread(row_owner * row_cap + row_rank, row_local, LANES)
    col_table = spread(col_owner * col_cap + col_rank, col_local, LANES)
    tile = jnp.concatenate(
        [row_table[None], col_table[None], jnp.zeros((6, LANES), jnp.int32)], axis=0
    )
    tables = share_tile(tile, inner, narrow)
    want_cols = lax.dynamic_slice_in_dim(tables[:, 1], narrow_me * col_cap, col_cap, axis=1)

    def want_rows(ring):
        owner = ring * inner + inner_me
        return lax.dynamic_slice_in_dim(tables[:, 0], owner * row_cap, row_cap, axis=1)

    forward = [(w, (w + inner) % wide) for w in range(wide)]
    chunks = []
    raw = density
    for step in range(steps):
        following = lax.ppermute(raw, "wide", forward) if step < steps - 1 else None
        ring = (ring_me - step + steps) % steps
        chosen = select(raw, want_rows(ring), want_cols)
        chunks.append(exchange(chosen, inner, narrow))
        raw = following

    col_place = col_owner * cap + col_rank
    in_plane = row_owner % inner * (narrow * cap) + row_rank * col_cap
    owner_ring = row_owner // inner
    row_in = (ring_me - owner_ring + steps) % steps * (group * cap) + in_plane
    row_out = (ring_me - 1 - owner_ring + 2 * steps) % steps * (group * cap) + in_plane

    rho, moment_parts = density_points(
        basis_lists, row_in, col_place, point_counts, orbitals, harmonics, weights, chunks
    )
    components = harmonics.shape[1]
    local = jnp.sum(moment_parts, axis=1)
    tile = jnp.zeros((8, LANES), jnp.float32).at[0, :components].set(local)
    moments = total_over_devices(tile, devices, narrow)[0, :components].reshape(components, 1)

    total_points = orbitals.shape[0] * orbitals.shape[2] * devices
    parts = integrals(
        basis_lists,
        row_out,
        col_place,
        point_counts,
        orbitals,
        harmonics,
        weights,
        rho,
        moments,
        steps,
        steps * group * cap,
        math.sqrt(total_points * components),
    )
    running = None
    for step in range(steps):
        got = exchange(parts[step].reshape(group, cap, BLK, BLK), inner, narrow)
        ring = (ring_me - 1 - step + 2 * steps) % steps
        last = step == steps - 1
        running = combine(
            got,
            running,
            want_rows(ring),
            want_cols,
            density.shape,
            jnp.float32 if last else jnp.bfloat16,
        )
        if not last:
            running = lax.ppermute(running, "wide", forward)
    return running


def solution(mesh):
    devices = mesh.shape["wide"] * mesh.shape["narrow"]

    def whole(density, block_slot, region_blocks, *others):
        region = region_blocks.shape[0] // devices
        in_specs = (
            P("wide", "narrow"),
            P(),
            P(("wide", "narrow")),
            P(("wide", "narrow"), None),
            P(("wide", "narrow")),
            P(("wide", "narrow"), None, None),
            P(("wide", "narrow"), None),
            P(("wide", "narrow"), None, None),
        )
        mapped = jax.shard_map(
            functools.partial(per_device, region),
            mesh=mesh,
            in_specs=in_specs,
            out_specs=P("wide", "narrow"),
            check_vma=False,
        )
        return mapped(density, block_slot, region_blocks, *others)

    return whole
```

time: 946 us -> 383 us (0.40)
  Pallas kernels: 0 us -> 310 us
  other arithmetic: 236 us -> 4.71 us
  blocking collectives: 230 us -> 0 us
  local copies, waits for them, and re-layouts: 200 us -> 8.88 us
  waiting for transfers between devices: 191 us -> 51.6 us
  matrix products: 71.7 us -> 0 us
    pallas_call x0 -> x20, Pallas kernels: none -> 310 us  [the longest x8 209 us: exchange(): pl.pallas_call(functools.partial(exchange_kernel, inner, narrow), out_sha...]
    scatter-add x13 -> x0, other arithmetic: 204 us -> none  [the longest x12 169 us: add_batch(): return (partial_h.at[list_row[:, None], list_row[None, :]].add(term), None)]
    all_to_all x2 -> x0, waiting for transfers between devices: 191 us -> none  [the longest x1 185 us: per_device(): lax.all_to_all(outgoing, ('wide', 'narrow'), split_axis=0, concat_axis=0,...]
    all_to_all x1 -> x0, blocking collectives: 189 us -> none  [per_device(): lax.all_to_all(send_back, ('wide', 'narrow'), split_axis=0, concat_axis=0...]
    gather x15 -> x0, local copies, waits for them, and re-layouts: 74.8 us -> none  [the longest x12 52.1 us: batch_density(): sub_matrix = region_density[list_row[:, None], list_row[None, :]]]
    dot_general x24 -> x0, matrix products: 71.7 us -> none  [the longest x12 48.3 us: add_batch(): jnp.einsum('aip,cjp->acij', scaled_rows, orb_rows, preferred_element_type...]
    transpose x12 -> x0, local copies, waits for them, and re-layouts: 64.1 us -> none  [add_batch(): jnp.einsum('aip,cjp->acij', scaled_rows, orb_rows, preferred_element_type...]
    ppermute x0 -> x6, waiting for transfers between devices: none -> 51.6 us  [the longest x3 49.6 us: per_device(): following = lax.ppermute(raw, 'wide', forward) if step < steps - 1 else None]
  transfers between devices with their start and end apart: 2 -> 6, of which waited for: 2 -> 5; matrix products, arithmetic and copies ran while one was open for 0% -> 2% of each run, Pallas kernels for 0% -> 47%
where the time goes in v1:
time: 383 us; the launch traced here: 381 us
  Pallas kernels  310 us (81%)
  waiting for transfers between devices  51.6 us (13%)
  local copies, waits for them, and re-layouts  8.88 us (2%)
  starting transfers between devices  5.59 us (1%)
  other arithmetic  4.71 us (1%)
    pallas_call x8, Pallas kernels, exchange(): pl.pallas_call(functools.partial(exchange_kernel, inner, narrow), out_sha...  209 us
    ppermute x3, waiting for transfers between devices, per_device(): following = lax.ppermute(raw, 'wide', forward) if step < steps - 1 else None  49.6 us
    pallas_call x4, Pallas kernels, combine(): pl.pallas_call(functools.partial(combine_kernel, row_cap, col_cap, prev i...  27.3 us
    pallas_call x4, Pallas kernels, select(): pl.pallas_call(functools.partial(select_kernel, row_cap, col_cap), out_sh...  20.8 us
    pallas_call x1, Pallas kernels, integrals(): pl.pallas_call(functools.partial(integral_kernel, steps, list_len, far_sc...  19.6 us
    pallas_call x1, Pallas kernels, density_points(): pl.pallas_call(functools.partial(density_kernel, steps, list_len), out_sh...  16.8 us
    pallas_call x1, Pallas kernels, total_over_devices(): pl.pallas_call(functools.partial(total_kernel, devices, narrow), out_shap...  11 us
  transfers between devices with their start and end apart: 6, of which 5 were waited for; matrix products, arithmetic and copies ran while one was open for 2% of the time, Pallas kernels for 47%

profile of v1, /device:TPU:0, one launch (start us, length us, event | category | flops | bytes accessed | tf_op | source)
XLA Modules:
  0.0 381.4 jit_solution(7631087142256911399)
XLA Ops:
  0.0 3.1 collective-permute-start
  3.1 25.4 %collective-permute-done.dens_ref = bf16[512,1024]{1,0:T(8,128)(2,1)S(1)} collective-permute-done((bf16[512,1024]{1,0:T(8,128)(2,1)}, bf16[512,1024]{1,0:T(8,128)(2,1)S(1)}, u32[]{:S(2)}, u32[]{:S(2)}) %collective-permute-start) | collective-permute-done | bytes 1048608 | tf_op jit(solution)/shard_map/ppermute | solution.py:491
  28.4 0.9 select_reduce_fusion.2
  29.4 0.2 convert_reduce_fusion.1
  29.6 0.2 convert_reduce_fusion
  29.7 0.6 fusion.7
  30.3 24.2 %collective-permute-done.1.dens_ref = bf16[512,1024]{1,0:T(8,128)(2,1)S(1)} collective-permute-done((bf16[512,1024]{1,0:T(8,128)(2,1)S(1)}, bf16[512,1024]{1,0:T(8,128)(2,1)S(1)}, u32[]{:S(2)}, u32[]{:S(2)}) %collective-permute-start.1) | collective-permute-done | bytes 1048608 | tf_op jit(solution)/shard_map/ppermute | solution.py:491
  54.6 0.6 multiply_add_fusion
  55.4 0.7 add_add_fusion.tile_ref
  56.0 5.9 %share_tile.1 = s32[8,8,128]{2,1,0:T(8,128)} custom-call(s32[8,128]{1,0:T(8,128)} %add_add_fusion.tile_ref), custom_call_target="tpu_custom_call" | custom-call | tf_op jit(solution)/shard_map/share_tile/pallas_call | solution.py:59
  62.0 0.8 fusion.11
  62.8 0.7 constant_dynamic-slice_fusion.6
  63.5 0.7 constant_dynamic-slice_fusion
  64.2 5.2 %select.117.src_ref = bf16[8,8,128,128]{3,2,1,0:T(8,128)(2,1)} custom-call(s32[8,2]{1,0:T(8,128)} %bitcast.37, s32[8,4]{1,0:T(8,128)} %bitcast.29, bf16[512,1024]{1,0:T(8,128)(2,1)} %dens_ref.1), custom_call_target="tpu_custom_call" | custom-call | tf_op jit(solution)/shard_map/select/pallas_call | solution.py:191
  69.5 25.7 %exchange.8 = bf16[8,8,128,128]{3,2,1,0:T(8,128)(2,1)} custom-call(bf16[8,8,128,128]{3,2,1,0:T(8,128)(2,1)} %select.117.src_ref), custom_call_target="tpu_custom_call" | custom-call | bytes 67108864 | tf_op jit(solution)/shard_map/exchange/pallas_call | solution.py:102
  95.2 0.7 copy.50.lists_ref
  95.9 0.5 fusion.3.row_ref
  96.4 5.2 %select.118.src_ref = bf16[8,8,128,128]{3,2,1,0:T(8,128)(2,1)} custom-call(s32[8,2]{1,0:T(8,128)} %bitcast.42, s32[8,4]{1,0:T(8,128)} %bitcast.30, bf16[512,1024]{1,0:T(8,128)(2,1)} %copy-done.1), custom_call_target="tpu_custom_call" | custom-call | tf_op jit(solution)/shard_map/select/pallas_call | solution.py:191
  101.6 26.2 %exchange.9 = bf16[8,8,128,128]{3,2,1,0:T(8,128)(2,1)} custom-call(bf16[8,8,128,128]{3,2,1,0:T(8,128)(2,1)} %select.118.src_ref), custom_call_target="tpu_custom_call" | custom-call | bytes 67108864 | tf_op jit(solution)/shard_map/exchange/pallas_call | solution.py:102
  127.9 5.2 %select.119.src_ref = bf16[8,8,128,128]{3,2,1,0:T(8,128)(2,1)} custom-call(s32[8,2]{1,0:T(8,128)} %bitcast.41, s32[8,4]{1,0:T(8,128)} %bitcast.31, bf16[512,1024]{1,0:T(8,128)(2,1)} %copy-done), custom_call_target="tpu_custom_call" | custom-call | tf_op jit(solution)/shard_map/select/pallas_call | solution.py:191
  133.1 26.2 %exchange.10 = bf16[8,8,128,128]{3,2,1,0:T(8,128)(2,1)} custom-call(bf16[8,8,128,128]{3,2,1,0:T(8,128)(2,1)} %select.119.src_ref), custom_call_target="tpu_custom_call" | custom-call | bytes 67108864 | tf_op jit(solution)/shard_map/exchange/pallas_call | solution.py:102
  159.4 1.0 copy-done.2
  160.4 5.2 %select.120.src_ref = bf16[8,8,128,128]{3,2,1,0:T(8,128)(2,1)} custom-call(s32[8,2]{1,0:T(8,128)} %bitcast.40, s32[8,4]{1,0:T(8,128)} %bitcast.32, bf16[512,1024]{1,0:T(8,128)(2,1)} %copy-done.2), custom_call_target="tpu_custom_call" | custom-call | tf_op jit(solution)/shard_map/select/pallas_call | solution.py:191
  165.6 26.2 %exchange.11 = bf16[8,8,128,128]{3,2,1,0:T(8,128)(2,1)} custom-call(bf16[8,8,128,128]{3,2,1,0:T(8,128)(2,1)} %select.120.src_ref), custom_call_target="tpu_custom_call" | custom-call | bytes 67108864 | tf_op jit(solution)/shard_map/exchange/pallas_call | solution.py:102
  191.8 16.8 %density_points.1 = (f32[12,256]{1,0:T(8,128)}, f32[64,256]{1,0:T(8,128)}) custom-call(s32[12,8]{1,0:T(8,128)} %copy.50.lists_ref, s32[16]{0:T(128)} %get-tuple-element.29.row_ref, s32[16]{0:T(128)} %get-tuple-element.41.col_ref, s32[12]{0:T(128)} %counts_ref.3, bf16[12,1024,256]{2,1,0:T(8,128)(2,1)} %orb_ref.3, bf16[12,64,256]{2,1,0:T(8,128)(2,1)} %harm_ref.3, ...), custom_call_target="tpu_custom_call" | custom-call | tf_op jit(solution)/shard_map/density_points/pallas_call | solution.py:315
  208.7 0.9 reduce_sum.59
  209.6 0.6 scatter.4.tile_ref
  210.2 11.0 %total_over_devices.1 = f32[8,128]{1,0:T(8,128)} custom-call(f32[8,128]{1,0:T(8,128)} %scatter.4.tile_ref), custom_call_target="tpu_custom_call" | custom-call | tf_op jit(solution)/shard_map/total_over_devices/pallas_call | solution.py:163
  221.3 0.7 slice_bitcast_fusion
  221.9 0.7 copy.51.moment_ref
  222.6 19.6 %integrals.1 = (bf16[64,128,128]{2,1,0:T(8,128)(2,1)}, bf16[64,128,128]{2,1,0:T(8,128)(2,1)}, bf16[64,128,128]{2,1,0:T(8,128)(2,1)}, bf16[64,128,128]{2,1,0:T(8,128)(2,1)}) custom-call(s32[12,8]{1,0:T(8,128)} %copy.50.lists_ref, s32[16]{0:T(128)} %fusion.3.row_ref, s32[16]{0:T(128)} %get-tuple-element.41.col_ref, s32[12]{0:T(128)} %counts_ref.3, ...), custom_call_target="tpu_custom_call" | custom-call | tf_op jit(solution)/shard_map/integrals/pallas_call | solution.py:415
  242.2 26.6 %exchange.15.got_ref = bf16[8,8,128,128]{3,2,1,0:T(8,128)(2,1)} custom-call(bf16[8,8,128,128]{3,2,1,0:T(8,128)(2,1)} %bitcast.28), custom_call_target="tpu_custom_call" | custom-call | bytes 67108864 | tf_op jit(solution)/shard_map/exchange/pallas_call | solution.py:102
  268.8 6.4 %combine.4 = bf16[512,1024]{1,0:T(8,128)(2,1)} custom-call(s32[8,2]{1,0:T(8,128)} %bitcast.39, s32[8,4]{1,0:T(8,128)} %bitcast.33, bf16[8,8,128,128]{3,2,1,0:T(8,128)(2,1)} %exchange.15.got_ref), custom_call_target="tpu_custom_call" | custom-call | tf_op jit(solution)/shard_map/combine/pallas_call | solution.py:242
  275.2 1.0 collective-permute-start.3
  276.2 26.0 %exchange.14.got_ref = bf16[8,8,128,128]{3,2,1,0:T(8,128)(2,1)} custom-call(bf16[8,8,128,128]{3,2,1,0:T(8,128)(2,1)} %bitcast.27), custom_call_target="tpu_custom_call" | custom-call | bytes 67108864 | tf_op jit(solution)/shard_map/exchange/pallas_call | solution.py:102
  302.2 0.9 collective-permute-done.3.rest_0_
  303.0 1.0 copy-done.5
  304.0 6.9 %combine.5 = bf16[512,1024]{1,0:T(8,128)(2,1)} custom-call(s32[8,2]{1,0:T(8,128)} %bitcast.44, s32[8,4]{1,0:T(8,128)} %bitcast.34, bf16[8,8,128,128]{3,2,1,0:T(8,128)(2,1)} %exchange.14.got_ref, bf16[512,1024]{1,0:T(8,128)(2,1)} %copy-done.5), custom_call_target="tpu_custom_call" | custom-call | tf_op jit(solution)/shard_map/combine/pallas_call | solution.py:242
  310.9 0.5 collective-permute-start.4
  311.4 26.0 %exchange.13.got_ref = bf16[8,8,128,128]{3,2,1,0:T(8,128)(2,1)} custom-call(bf16[8,8,128,128]{3,2,1,0:T(8,128)(2,1)} %bitcast.26), custom_call_target="tpu_custom_call" | custom-call | bytes 67108864 | tf_op jit(solution)/shard_map/exchange/pallas_call | solution.py:102
  337.4 0.8 collective-permute-done.4.rest_0_
  338.1 1.0 copy-done.4
  339.1 6.8 %combine.6 = bf16[512,1024]{1,0:T(8,128)(2,1)} custom-call(s32[8,2]{1,0:T(8,128)} %bitcast.43, s32[8,4]{1,0:T(8,128)} %bitcast.35, bf16[8,8,128,128]{3,2,1,0:T(8,128)(2,1)} %exchange.13.got_ref, bf16[512,1024]{1,0:T(8,128)(2,1)} %copy-done.4), custom_call_target="tpu_custom_call" | custom-call | tf_op jit(solution)/shard_map/combine/pallas_call | solution.py:242
  345.9 1.0 collective-permute-start.5
  346.9 26.0 %exchange.12.got_ref = bf16[8,8,128,128]{3,2,1,0:T(8,128)(2,1)} custom-call(bf16[8,8,128,128]{3,2,1,0:T(8,128)(2,1)} %bitcast.25), custom_call_target="tpu_custom_call" | custom-call | bytes 67108864 | tf_op jit(solution)/shard_map/exchange/pallas_call | solution.py:102
  372.9 0.4 collective-permute-done.5.rest_0_
  373.3 1.0 copy-done.3
  374.2 7.2 %combine.7 = f32[512,1024]{1,0:T(8,128)} custom-call(s32[8,2]{1,0:T(8,128)} %bitcast.38, s32[8,4]{1,0:T(8,128)} %bitcast.36, bf16[8,8,128,128]{3,2,1,0:T(8,128)(2,1)} %exchange.12.got_ref, bf16[512,1024]{1,0:T(8,128)(2,1)} %copy-done.3), custom_call_target="tpu_custom_call" | custom-call | tf_op jit(solution)/shard_map/combine/pallas_call | solution.py:242
  (17 shorter events, 0.2 us)
Async XLA Ops:
  0.0 28.4 %collective-permute-start = (bf16[512,1024]{1,0:T(8,128)(2,1)}, bf16[512,1024]{1,0:T(8,128)(2,1)S(1)}, u32[]{:S(2)}, u32[]{:S(2)}) collective-permute-start(bf16[512,1024]{1,0:T(8,128)(2,1)} %dens_ref.1), channel_id=1, source_target_pairs={{0,8},{4,12},{8,16},{12,20},{16,24},{20,28},{24,0},{28,4},{1,9},{5... | collective-permute-start | bytes 3145736 | tf_op jit(solution)/shard_map/ppermute | solution.py:491
  28.4 66.8 %copy-start.1 = (bf16[512,1024]{1,0:T(8,128)(2,1)}, bf16[512,1024]{1,0:T(8,128)(2,1)S(1)}, u32[]{:S(2)}) copy-start(bf16[512,1024]{1,0:T(8,128)(2,1)S(1)} %collective-permute-done.dens_ref) | copy-start | bytes 3145732
  28.4 26.1 %collective-permute-start.1 = (bf16[512,1024]{1,0:T(8,128)(2,1)S(1)}, bf16[512,1024]{1,0:T(8,128)(2,1)S(1)}, u32[]{:S(2)}, u32[]{:S(2)}) collective-permute-start(bf16[512,1024]{1,0:T(8,128)(2,1)S(1)} %collective-permute-done.dens_ref), channel_id=1, source_target_pairs={{0,8},{4,12},{8,16},{12,20},{16,24},{20,28},{24,0},{28,4},{1,9},{5... | collective-permute-start | bytes 3145736 | tf_op jit(solution)/shard_map/ppermute | solution.py:491
  54.6 40.6 %copy-start = (bf16[512,1024]{1,0:T(8,128)(2,1)}, bf16[512,1024]{1,0:T(8,128)(2,1)S(1)}, u32[]{:S(2)}) copy-start(bf16[512,1024]{1,0:T(8,128)(2,1)S(1)} %collective-permute-done.1.dens_ref) | copy-start | bytes 3145732
  54.6 104.8 %collective-permute-start.2 = (bf16[512,1024]{1,0:T(8,128)(2,1)S(1)}, bf16[512,1024]{1,0:T(8,128)(2,1)S(1)}, u32[]{:S(2)}, u32[]{:S(2)}) collective-permute-start(bf16[512,1024]{1,0:T(8,128)(2,1)S(1)} %collective-permute-done.1.dens_ref), channel_id=1, source_target_pairs={{0,8},{4,12},{8,16},{12,20},{16,24},{20,28},{24,0},{28,4},{1,9},{5... | collective-permute-start | bytes 3145736 | tf_op jit(solution)/shard_map/ppermute | solution.py:491
  69.5 25.8 %copy-start.6 = (s32[12,8]{0,1:T(8,128)S(1)}, s32[12,8]{0,1:T(8,128)}, u32[]{:S(2)}) copy-start(s32[12,8]{0,1:T(8,128)} %param.13) | copy-start | bytes 1156
  159.4 1.0 copy-start.2
  275.2 27.8 %collective-permute-start.3 = (bf16[512,1024]{1,0:T(8,128)(2,1)}, bf16[512,1024]{1,0:T(8,128)(2,1)S(1)}, u32[]{:S(2)}, u32[]{:S(2)}) collective-permute-start(bf16[512,1024]{1,0:T(8,128)(2,1)} %combine.4), channel_id=1, source_target_pairs={{0,8},{4,12},{8,16},{12,20},{16,24},{20,28},{24,0},{28,4},{1,9},{5... | collective-permute-start | bytes 3145736 | tf_op jit(solution)/shard_map/ppermute | solution.py:540
  303.0 1.0 copy-start.5
  310.9 27.3 %collective-permute-start.4 = (bf16[512,1024]{1,0:T(8,128)(2,1)}, bf16[512,1024]{1,0:T(8,128)(2,1)S(1)}, u32[]{:S(2)}, u32[]{:S(2)}) collective-permute-start(bf16[512,1024]{1,0:T(8,128)(2,1)} %combine.5), channel_id=1, source_target_pairs={{0,8},{4,12},{8,16},{12,20},{16,24},{20,28},{24,0},{28,4},{1,9},{5... | collective-permute-start | bytes 3145736 | tf_op jit(solution)/shard_map/ppermute | solution.py:540
  338.1 1.0 copy-start.4
  345.9 27.3 %collective-permute-start.5 = (bf16[512,1024]{1,0:T(8,128)(2,1)}, bf16[512,1024]{1,0:T(8,128)(2,1)S(1)}, u32[]{:S(2)}, u32[]{:S(2)}) collective-permute-start(bf16[512,1024]{1,0:T(8,128)(2,1)} %combine.6), channel_id=1, source_target_pairs={{0,8},{4,12},{8,16},{12,20},{16,24},{20,28},{24,0},{28,4},{1,9},{5... | collective-permute-start | bytes 3145736 | tf_op jit(solution)/shard_map/ppermute | solution.py:540
  373.3 1.0 copy-start.3

commit v2 on v1

--- a/solution.py
+++ b/solution.py
@@ -70,54 +70,6 @@
     )(tile)
 
 
-def exchange_kernel(inner, narrow, src_ref, out_ref, own, send_sem, recv_sem, own_sem):
-    mine, _, _ = plane_peer(0, inner, narrow)
-    take = pltpu.make_async_copy(src_ref.at[mine], own, own_sem.at[0])
-    take.start()
-    plane_barrier(inner, narrow)
-    copies = []
-    for offset in range(1, inner * narrow):
-        _, other, device = plane_peer(offset, inner, narrow)
-        copy = pltpu.make_async_remote_copy(
-            src_ref=src_ref.at[other],
-            dst_ref=out_ref.at[mine],
-            send_sem=send_sem.at[offset - 1],
-            recv_sem=recv_sem.at[offset - 1],
-            device_id=device,
-            device_id_type=MESH,
-        )
-        copy.start()
-        copies.append(copy)
-    take.wait()
-    put = pltpu.make_async_copy(own, out_ref.at[mine], own_sem.at[1])
-    put.start()
-    put.wait()
-    for copy in copies:
-        copy.wait()
-
-
-def exchange(blocks, inner, narrow):
-    group = inner * narrow
-    size = math.prod(blocks.shape) * 2
-    return pl.pallas_call(
-        functools.partial(exchange_kernel, inner, narrow),
-        out_shape=jax.ShapeDtypeStruct(blocks.shape, blocks.dtype),
-        in_specs=[pl.BlockSpec(memory_space=pl.ANY)],
-        out_specs=pl.BlockSpec(memory_space=pl.ANY),
-        scratch_shapes=[
-            pltpu.VMEM(blocks.shape[1:], blocks.dtype),
-            pltpu.SemaphoreType.DMA((group - 1,)),
-            pltpu.SemaphoreType.DMA((group - 1,)),
-            pltpu.SemaphoreType.DMA((2,)),
-        ],
-        compiler_params=pltpu.CompilerParams(collective_id=1, has_side_effects=True),
-        cost_estimate=pl.CostEstimate(
-            flops=0, bytes_accessed=size * 32, transcendentals=0
-        ),
-        name="exchange",
-    )(blocks)
-
-
 def total_kernel(devices, narrow, tile_ref, out_ref, held, send_sem, recv_sem):
     mine = lax.axis_index("wide") * narrow + lax.axis_index("narrow")
 
@@ -175,83 +127,306 @@
     )(tile)
 
 
-def select_kernel(row_cap, col_cap, rows_ref, cols_ref, dens_ref, out_ref):
-    dest = pl.program_id(0)
-    for rr in range(row_cap):
-        row = pl.multiple_of(rows_ref[dest, rr] * BLK, BLK)
-        for cr in range(col_cap):
-            col = pl.multiple_of(cols_ref[dest, cr] * BLK, BLK)
-            out_ref[0, rr * col_cap + cr] = dens_ref[pl.ds(row, BLK), pl.ds(col, BLK)]
-
-
-def select(dens, rows, cols):
-    group, row_cap = rows.shape
-    col_cap = cols.shape[1]
+def ring_device(shift, inner):
+    wide = lax.axis_size("wide")
+    return (lax.rem(lax.axis_index("wide") + shift * inner + wide, wide), lax.axis_index("narrow"))
+
+
+def entry_barrier(steps, inner, narrow):
+    barrier = pltpu.get_barrier_semaphore()
+    group = inner * narrow
+
+    def greet(offset, carry):
+        _, _, device = plane_peer(offset, inner, narrow)
+        pl.semaphore_signal(barrier, inc=1, device_id=device, device_id_type=MESH)
+        return carry
+
+    lax.fori_loop(1, group, greet, 0)
+    if steps > 1:
+        for shift in (1, -1):
+            pl.semaphore_signal(
+                barrier, inc=1, device_id=ring_device(shift, inner), device_id_type=MESH
+            )
+    pl.semaphore_wait(barrier, group - 1 + (2 if steps > 1 else 0))
+
+
+def gather_kernel(steps, inner, narrow, row_cap, col_cap, rows_ref, cols_ref, dens_ref, *rest):
+    outs, rest = rest[:steps], rest[steps:]
+    raws, rest = rest[:steps], rest[steps:]
+    chosen, send_sem, recv_sem, ring_send, ring_recv, own_sem, load_sem = rest
+    group = inner * narrow
+    ring_me = lax.axis_index("wide") // inner
+    mine, _, _ = plane_peer(0, inner, narrow)
+    col_blocks = dens_ref.shape[1] // BLK
+    held = raws[0].shape[0]
+    half = held // 2
+
+    def load_copy(place):
+        row, col = place // col_blocks, place % col_blocks
+        return pltpu.make_async_copy(
+            dens_ref.at[
+                pl.ds(pl.multiple_of(row * BLK, BLK), BLK),
+                pl.ds(pl.multiple_of(col * BLK, BLK), BLK),
+            ],
+            raws[0].at[place],
+            load_sem.at[place],
+        )
+
+    def load(place, carry):
+        load_copy(place).start()
+        return carry
+
+    def loaded(place, carry):
+        load_copy(place).wait()
+        return carry
+
+    def pick(step):
+        ring = lax.rem(ring_me - step + steps, steps)
+
+        def body(offset, carry):
+            _, other, _ = plane_peer(offset, inner, narrow)
+            for rr in range(row_cap):
+                row = rows_ref[other, ring * row_cap + rr] * col_blocks
+                for cr in range(col_cap):
+                    place = row + cols_ref[other, cr]
+                    chosen[step, offset, rr * col_cap + cr] = raws[step][place]
+            return carry
+
+        lax.fori_loop(0, group, body, 0)
+
+    def block_copy(step, offset):
+        _, _, device = plane_peer(offset, inner, narrow)
+        return pltpu.make_async_remote_copy(
+            src_ref=chosen.at[step, offset],
+            dst_ref=outs[step].at[mine],
+            send_sem=send_sem.at[step, offset - 1],
+            recv_sem=recv_sem.at[step, offset - 1],
+            device_id=device,
+            device_id_type=MESH,
+        )
+
+    def ring_copy(step, piece):
+        span = pl.ds(piece * half, half)
+        return pltpu.make_async_remote_copy(
+            src_ref=raws[step].at[span],
+            dst_ref=raws[step + 1].at[span],
+            send_sem=ring_send.at[step, piece],
+            recv_sem=ring_recv.at[step, piece],
+            device_id=ring_device(1, inner),
+            device_id_type=MESH,
+        )
+
+    def own_copy(step):
+        return pltpu.make_async_copy(chosen.at[step, 0], outs[step].at[mine], own_sem.at[step])
+
+    for step in range(steps):
+        if step == 0:
+            lax.fori_loop(0, held, load, 0)
+            lax.fori_loop(0, held, loaded, 0)
+            pick(0)
+            entry_barrier(steps, inner, narrow)
+        for piece in range(2):
+            if step > 0:
+                ring_copy(step - 1, piece).wait_recv()
+            if step < steps - 1:
+                ring_copy(step, piece).start()
+        if step > 0:
+            pick(step)
+
+        def send(offset, carry, step=step):
+            block_copy(step, offset).start()
+            return carry
+
+        lax.fori_loop(1, group, send, 0)
+        own_copy(step).start()
+    for step in range(steps):
+
+        def finish(offset, carry, step=step):
+            block_copy(step, offset).wait()
+            return carry
+
+        lax.fori_loop(1, group, finish, 0)
+        own_copy(step).wait()
+        if step < steps - 1:
+            for piece in range(2):
+                ring_copy(step, piece).wait_send()
+
+
+def gather_blocks(dens, rows, cols, steps, inner, narrow, row_cap, col_cap):
+    group = inner * narrow
     cap = row_cap * col_cap
+    ring_sems = max(1, steps - 1)
+    held = dens.shape[0] // BLK * (dens.shape[1] // BLK)
     return pl.pallas_call(
-        functools.partial(select_kernel, row_cap, col_cap),
-        out_shape=jax.ShapeDtypeStruct((group, cap, BLK, BLK), dens.dtype),
-        grid_spec=pltpu.PrefetchScalarGridSpec(
-            num_scalar_prefetch=2,
-            grid=(group,),
-            in_specs=[pl.BlockSpec(dens.shape, lambda g, *_: (0, 0))],
-            out_specs=pl.BlockSpec((1, cap, BLK, BLK), lambda g, *_: (g, 0, 0, 0)),
+        functools.partial(gather_kernel, steps, inner, narrow, row_cap, col_cap),
+        out_shape=[jax.ShapeDtypeStruct((group, cap, BLK, BLK), dens.dtype)] * steps,
+        in_specs=[
+            pl.BlockSpec(memory_space=pltpu.SMEM),
+            pl.BlockSpec(memory_space=pltpu.SMEM),
+            pl.BlockSpec(memory_space=pl.ANY),
+        ],
+        out_specs=[pl.BlockSpec(memory_space=pl.ANY)] * steps,
+        scratch_shapes=[pltpu.VMEM((held, BLK, BLK), dens.dtype)] * steps
+        + [
+            pltpu.VMEM((steps, group, cap, BLK, BLK), dens.dtype),
+            pltpu.SemaphoreType.DMA((steps, group - 1)),
+            pltpu.SemaphoreType.DMA((steps, group - 1)),
+            pltpu.SemaphoreType.DMA((ring_sems, 2)),
+            pltpu.SemaphoreType.DMA((ring_sems, 2)),
+            pltpu.SemaphoreType.DMA((steps,)),
+            pltpu.SemaphoreType.DMA((held,)),
+        ],
+        compiler_params=pltpu.CompilerParams(
+            collective_id=1, has_side_effects=True, vmem_limit_bytes=VMEM_BYTES
         ),
-        compiler_params=pltpu.CompilerParams(vmem_limit_bytes=VMEM_BYTES),
-        name="select",
+        name="gather_blocks",
     )(rows, cols, dens)
 
 
-def combine_kernel(row_cap, col_cap, has_prev, rows_ref, cols_ref, got_ref, *rest):
-    if has_prev:
-        prev_ref, out_ref, acc = rest
-    else:
-        prev_ref, (out_ref, acc) = None, rest
-    source = pl.program_id(0)
-
-    @pl.when(source == 0)
-    def _():
-        if has_prev:
-            acc[...] = prev_ref[...].astype(jnp.float32)
-        else:
-            acc[...] = jnp.zeros_like(acc)
-
-    for rr in range(row_cap):
-        row = pl.multiple_of(rows_ref[source, rr] * BLK, BLK)
-        for cr in range(col_cap):
-            col = pl.multiple_of(cols_ref[source, cr] * BLK, BLK)
-            acc[pl.ds(row, BLK), pl.ds(col, BLK)] += got_ref[
-                0, rr * col_cap + cr
-            ].astype(jnp.float32)
-
-    @pl.when(source == pl.num_programs(0) - 1)
-    def _():
-        out_ref[...] = acc[...].astype(out_ref.dtype)
-
-
-def combine(got, prev, rows, cols, shape, dtype):
-    group, row_cap = rows.shape
-    col_cap = cols.shape[1]
-    cap = row_cap * col_cap
-    whole = pl.BlockSpec(shape, lambda g, *_: (0, 0))
-    specs = [pl.BlockSpec((1, cap, BLK, BLK), lambda g, *_: (g, 0, 0, 0))]
-    operands = [got]
-    if prev is not None:
-        specs.append(whole)
-        operands.append(prev)
+def return_kernel(steps, inner, narrow, cap, rows_ref, cols_ref, *rest):
+    parts, rest = rest[:steps], rest[steps:]
+    out_ref, rest = rest[0], rest[1:]
+    gots, rest = rest[:steps], rest[steps:]
+    runs, rest = rest[: steps - 1], rest[steps - 1 :]
+    prevs, rest = (None,) + rest[: steps - 1], rest[steps - 1 :]
+    send_sem, recv_sem, ring_send, ring_recv, own_sem = rest
+    group = inner * narrow
+    ring_me = lax.axis_index("wide") // inner
+    mine, _, _ = plane_peer(0, inner, narrow)
+    row_blocks = out_ref.shape[0] // BLK
+    col_blocks = out_ref.shape[1] // BLK
+    empty = group * cap
+
+    def block_copy(step, offset):
+        _, other, device = plane_peer(offset, inner, narrow)
+        return pltpu.make_async_remote_copy(
+            src_ref=parts[step].at[pl.ds(other * cap, cap)],
+            dst_ref=gots[step].at[pl.ds(mine * cap, cap)],
+            send_sem=send_sem.at[step, offset - 1],
+            recv_sem=recv_sem.at[step, offset - 1],
+            device_id=device,
+            device_id_type=MESH,
+        )
+
+    def own_copy(step):
+        span = pl.ds(mine * cap, cap)
+        return pltpu.make_async_copy(parts[step].at[span], gots[step].at[span], own_sem.at[step])
+
+    def ring_copy(step, piece):
+        span = pl.ds(piece * BLK, BLK)
+        return pltpu.make_async_remote_copy(
+            src_ref=runs[step].at[span],
+            dst_ref=prevs[step + 1].at[span],
+            send_sem=ring_send.at[step, piece],
+            recv_sem=ring_recv.at[step, piece],
+            device_id=ring_device(1, inner),
+            device_id_type=MESH,
+        )
+
+    def start_step(step):
+        own_copy(step).start()
+
+        def send(offset, carry):
+            block_copy(step, offset).start()
+            return carry
+
+        lax.fori_loop(1, group, send, 0)
+
+    for step in range(steps):
+        gots[step][empty] = jnp.zeros((BLK, BLK), gots[step].dtype)
+    entry_barrier(steps, inner, narrow)
+    for step in range(min(2, steps)):
+        start_step(step)
+    for step in range(steps):
+        last = step == steps - 1
+        ring = lax.rem(ring_me - 1 - step + 2 * steps, steps)
+
+        def arrive(offset, carry, step=step):
+            block_copy(step, offset).wait_recv()
+            return carry
+
+        lax.fori_loop(1, group, arrive, 0)
+        own_copy(step).wait()
+        if step + 2 < steps:
+            start_step(step + 2)
+
+        def add_row(piece, carry, step=step, last=last, ring=ring):
+            if step > 0:
+                ring_copy(step - 1, piece).wait_recv()
+            span = pl.ds(pl.multiple_of(piece * BLK, BLK), BLK)
+            bases = [
+                rows_ref[source, ring * row_blocks + piece] + source * cap
+                for source in range(group)
+            ]
+
+            def add_block(block, inner_carry):
+                across = pl.ds(pl.multiple_of(block * BLK, BLK), BLK)
+                if step > 0:
+                    total = prevs[step][span, across].astype(jnp.float32)
+                else:
+                    total = jnp.zeros((BLK, BLK), jnp.float32)
+                for source in range(group):
+                    place = jnp.minimum(bases[source] + cols_ref[source, block], empty)
+                    total += gots[step][place].astype(jnp.float32)
+                if last:
+                    out_ref[span, across] = total
+                else:
+                    runs[step][span, across] = total.astype(runs[step].dtype)
+                return inner_carry
+
+            lax.fori_loop(0, col_blocks, add_block, 0)
+            if not last:
+
+                @pl.when(piece > 0)
+                def _():
+                    ring_copy(step, piece - 1).start()
+
+            return carry
+
+        lax.fori_loop(0, row_blocks, add_row, 0)
+        if not last:
+            ring_copy(step, row_blocks - 1).start()
+    for step in range(steps):
+
+        def finish(offset, carry, step=step):
+            block_copy(step, offset).wait_send()
+            return carry
+
+        lax.fori_loop(1, group, finish, 0)
+        if step < steps - 1:
+
+            def left(piece, carry, step=step):
+                ring_copy(step, piece).wait_send()
+                return carry
+
+            lax.fori_loop(0, row_blocks, left, 0)
+
+
+def return_blocks(parts, rows, cols, shape, steps, inner, narrow, cap):
+    group = inner * narrow
+    ring_sems = max(1, steps - 1)
+    row_blocks = shape[0] // BLK
+    dtype = parts[0].dtype
     return pl.pallas_call(
-        functools.partial(combine_kernel, row_cap, col_cap, prev is not None),
-        out_shape=jax.ShapeDtypeStruct(shape, dtype),
-        grid_spec=pltpu.PrefetchScalarGridSpec(
-            num_scalar_prefetch=2,
-            grid=(group,),
-            in_specs=specs,
-            out_specs=whole,
-            scratch_shapes=[pltpu.VMEM(shape, jnp.float32)],
+        functools.partial(return_kernel, steps, inner, narrow, cap),
+        out_shape=jax.ShapeDtypeStruct(shape, jnp.float32),
+        in_specs=[pl.BlockSpec(memory_space=pltpu.SMEM)] * 2
+        + [pl.BlockSpec(memory_space=pl.ANY)] * steps,
+        out_specs=pl.BlockSpec(memory_space=pltpu.VMEM),
+        scratch_shapes=[pltpu.VMEM((group * cap + 1, BLK, BLK), dtype)] * steps
+        + [pltpu.VMEM(shape, dtype)] * (2 * (steps - 1))
+        + [
+            pltpu.SemaphoreType.DMA((steps, group - 1)),
+            pltpu.SemaphoreType.DMA((steps, group - 1)),
+            pltpu.SemaphoreType.DMA((ring_sems, row_blocks)),
+            pltpu.SemaphoreType.DMA((ring_sems, row_blocks)),
+            pltpu.SemaphoreType.DMA((steps,)),
+        ],
+        compiler_params=pltpu.CompilerParams(
+            collective_id=3, has_side_effects=True, vmem_limit_bytes=VMEM_BYTES
         ),
-        compiler_params=pltpu.CompilerParams(vmem_limit_bytes=VMEM_BYTES),
-        name="combine",
-    )(rows, cols, *operands)
+        name="return_blocks",
+    )(rows, cols, *parts)
 
 
 def live_row(weights_ref, counts_ref, batch):
@@ -474,25 +649,34 @@
     row_rank, col_rank = rank_among(row_owner), rank_among(col_owner)
     row_table = spread(row_owner * row_cap + row_rank, row_local, LANES)
     col_table = spread(col_owner * col_cap + col_rank, col_local, LANES)
-    tile = jnp.concatenate(
-        [row_table[None], col_table[None], jnp.zeros((6, LANES), jnp.int32)], axis=0
+    far = 1 << 20
+    row_blocks = density.shape[0] // BLK
+    col_blocks = density.shape[1] // BLK
+    row_back = far + spread(
+        row_owner * row_blocks + row_local, row_rank * col_cap - far, LANES
     )
+    col_back = far + spread(col_owner * col_blocks + col_local, col_rank - far, LANES)
+    tile = jnp.stack([row_table, col_table, row_back, col_back] * 2)
     tables = share_tile(tile, inner, narrow)
-    want_cols = lax.dynamic_slice_in_dim(tables[:, 1], narrow_me * col_cap, col_cap, axis=1)
-
-    def want_rows(ring):
-        owner = ring * inner + inner_me
-        return lax.dynamic_slice_in_dim(tables[:, 0], owner * row_cap, row_cap, axis=1)
-
-    forward = [(w, (w + inner) % wide) for w in range(wide)]
-    chunks = []
-    raw = density
-    for step in range(steps):
-        following = lax.ppermute(raw, "wide", forward) if step < steps - 1 else None
-        ring = (ring_me - step + steps) % steps
-        chosen = select(raw, want_rows(ring), want_cols)
-        chunks.append(exchange(chosen, inner, narrow))
-        raw = following
+
+    def rows_here(plane, each):
+        used = tables[:, plane, : wide * each].reshape(group, steps, inner, each)
+        one = lax.dynamic_index_in_dim(used, inner_me, axis=2, keepdims=False)
+        return one.reshape(group, steps * each)
+
+    def cols_here(plane, each):
+        return lax.dynamic_slice_in_dim(tables[:, plane], narrow_me * each, each, axis=1)
+
+    chunks = gather_blocks(
+        density,
+        rows_here(0, row_cap),
+        cols_here(1, col_cap),
+        steps,
+        inner,
+        narrow,
+        row_cap,
+        col_cap,
+    )
 
     col_place = col_owner * cap + col_rank
     in_plane = row_owner % inner * (narrow * cap) + row_rank * col_cap
@@ -523,22 +707,16 @@
         steps * group * cap,
         math.sqrt(total_points * components),
     )
-    running = None
-    for step in range(steps):
-        got = exchange(parts[step].reshape(group, cap, BLK, BLK), inner, narrow)
-        ring = (ring_me - 1 - step + 2 * steps) % steps
-        last = step == steps - 1
-        running = combine(
-            got,
-            running,
-            want_rows(ring),
-            want_cols,
-            density.shape,
-            jnp.float32 if last else jnp.bfloat16,
-        )
-        if not last:
-            running = lax.ppermute(running, "wide", forward)
-    return running
+    return return_blocks(
+        parts,
+        rows_here(2, row_blocks),
+        cols_here(3, col_blocks),
+        density.shape,
+        steps,
+        inner,
+        narrow,
+        cap,
+    )
 
 
 def solution(mesh):

time: 383 us -> 271 us (0.71)
  Pallas kernels: 310 us -> 251 us
  waiting for transfers between devices: 51.6 us -> 0 us
  starting transfers between devices: 5.59 us -> 0 us
    pallas_call x16 -> x2, Pallas kernels: 257 us -> 197 us  [the longest x1 100 us: gather_blocks(): pl.pallas_call(functools.partial(gather_kernel, steps, inner, narrow, row...]
    ppermute x6 -> x0, waiting for transfers between devices: 51.6 us -> none  [the longest x3 49.6 us: per_device(): following = lax.ppermute(raw, 'wide', forward) if step < steps - 1 else None]
    ppermute x6 -> x0, starting transfers between devices: 5.59 us -> none  [the longest x3 3.06 us: per_device(): following = lax.ppermute(raw, 'wide', forward) if step < steps - 1 else None]
  transfers between devices with their start and end apart: 6 -> 0, of which waited for: 5 -> 0; matrix products, arithmetic and copies ran while one was open for 2% -> 0% of each run, Pallas kernels for 47% -> 0%
where the time goes in v2:
time: 271 us; the launch traced here: 267 us
  Pallas kernels  251 us (93%)
  local copies, waits for them, and re-layouts  12.3 us (5%)
  other arithmetic  4.03 us (1%)
    pallas_call x1, Pallas kernels, gather_blocks(): pl.pallas_call(functools.partial(gather_kernel, steps, inner, narrow, row...  100 us
    pallas_call x1, Pallas kernels, return_blocks(): pl.pallas_call(functools.partial(return_kernel, steps, inner, narrow, cap...  96.2 us
    pallas_call x1, Pallas kernels, integrals(): pl.pallas_call(functools.partial(integral_kernel, steps, list_len, far_sc...  19.6 us
    pallas_call x1, Pallas kernels, density_points(): pl.pallas_call(functools.partial(density_kernel, steps, list_len), out_sh...  16.8 us
    pallas_call x1, Pallas kernels, total_over_devices(): pl.pallas_call(functools.partial(total_kernel, devices, narrow), out_shap...  10.3 us
    pallas_call x1, Pallas kernels, share_tile(): pl.pallas_call(functools.partial(tile_kernel, inner, narrow), out_shape=j...  7.54 us

profile of v2, /device:TPU:0, one launch (start us, length us, event | category | flops | bytes accessed | tf_op | source)
XLA Modules:
  0.0 267.3 jit_solution(11585858854631877567)
XLA Ops:
  0.0 0.9 select_reduce_fusion.4
  0.9 0.2 convert_reduce_fusion
  1.1 0.2 convert_reduce_fusion.1
  1.2 0.5 multiply_add_fusion.3
  1.7 0.6 fusion.7
  2.3 0.1 select_reduce_fusion
  2.4 0.1 select_reduce_fusion.2
  2.5 0.6 fusion.3.row_ref
  3.1 0.6 stack.8.tile_ref
  3.7 1.4 copy.33.lists_ref
  5.1 7.5 %share_tile.1 = s32[8,8,128]{2,1,0:T(8,128)} custom-call(s32[8,128]{1,0:T(8,128)} %stack.8.tile_ref), custom_call_target="tpu_custom_call" | custom-call | tf_op jit(solution)/shard_map/share_tile/pallas_call | solution.py:59
  12.6 0.8 slice.33
  13.4 0.1 copy.28
  13.5 0.7 copy.30.rows_ref
  14.1 0.8 slice.31
  14.9 0.8 fusion.11
  15.7 0.7 constant_dynamic-slice_fusion.3
  16.4 0.7 constant_dynamic-slice_fusion.1
  17.1 0.1 copy.27
  17.1 0.7 copy.35.rows_ref
  17.8 100.4 %gather_blocks.1 = (bf16[8,8,128,128]{3,2,1,0:T(8,128)(2,1)}, bf16[8,8,128,128]{3,2,1,0:T(8,128)(2,1)}, bf16[8,8,128,128]{3,2,1,0:T(8,128)(2,1)}, bf16[8,8,128,128]{3,2,1,0:T(8,128)(2,1)}) custom-call(s32[8,8]{1,0:T(8,128)} %copy.30.rows_ref, s32[8,4]{1,0:T(8,128)} %bitcast.27, bf16[512,1024]{1,0:T(8,128)(2,1)} %dens_ref.1), custom_call_target="tpu_custom_call" | custom-call | tf_op jit(solution)/shard_map/gather_blocks/pallas_call | solution.py:260
  118.3 16.8 %density_points.1 = (f32[12,256]{1,0:T(8,128)}, f32[64,256]{1,0:T(8,128)}) custom-call(s32[12,8]{1,0:T(8,128)} %copy.33.lists_ref, s32[16]{0:T(128)} %get-tuple-element.37.row_ref, s32[16]{0:T(128)} %get-tuple-element.48.col_ref, s32[12]{0:T(128)} %counts_ref.3, bf16[12,1024,256]{2,1,0:T(8,128)(2,1)} %orb_ref.3, bf16[12,64,256]{2,1,0:T(8,128)(2,1)} %harm_ref.3, ...), custom_call_target="tpu_custom_call" | custom-call | tf_op jit(solution)/shard_map/density_points/pallas_call | solution.py:490
  135.1 0.9 reduce_sum.79
  136.1 0.6 scatter.4.tile_ref
  136.7 10.3 %total_over_devices.1 = f32[8,128]{1,0:T(8,128)} custom-call(f32[8,128]{1,0:T(8,128)} %scatter.4.tile_ref), custom_call_target="tpu_custom_call" | custom-call | tf_op jit(solution)/shard_map/total_over_devices/pallas_call | solution.py:115
  147.0 0.7 slice_bitcast_fusion
  147.6 0.7 copy.34.moment_ref
  148.3 19.6 %integrals.1 = (bf16[64,128,128]{2,1,0:T(8,128)(2,1)}, bf16[64,128,128]{2,1,0:T(8,128)(2,1)}, bf16[64,128,128]{2,1,0:T(8,128)(2,1)}, bf16[64,128,128]{2,1,0:T(8,128)(2,1)}) custom-call(s32[12,8]{1,0:T(8,128)} %copy.33.lists_ref, s32[16]{0:T(128)} %fusion.3.row_ref, s32[16]{0:T(128)} %get-tuple-element.48.col_ref, s32[12]{0:T(128)} %counts_ref.3, ...), custom_call_target="tpu_custom_call" | custom-call | tf_op jit(solution)/shard_map/integrals/pallas_call | solution.py:590
  167.9 96.2 %return_blocks.1 = f32[512,1024]{1,0:T(8,128)} custom-call(s32[8,16]{1,0:T(8,128)} %copy.35.rows_ref, s32[8,8]{1,0:T(8,128)} %bitcast.26, bf16[64,128,128]{2,1,0:T(8,128)(2,1)} %get-tuple-element.33.rest_0_, bf16[64,128,128]{2,1,0:T(8,128)(2,1)} %get-tuple-element.34.rest_1_, bf16[64,128,128]{2,1,0:T(8,128)(2,1)} %get-tuple-element.35.rest_2_, ...), custom_call_target="tpu_custom_call" | custom-call | tf_op jit(solution)/shard_map/return_blocks/pallas_call | solution.py:410
  264.2 3.2 %copy.38 = f32[512,1024]{1,0:T(8,128)} copy(f32[512,1024]{1,0:T(8,128)} %return_blocks.1) | data formatting | bytes 4194304
  (5 shorter events, 0.0 us)

commit v3 on v2

--- a/solution.py
+++ b/solution.py
@@ -25,108 +25,6 @@
     return mine, other, (base + other // narrow, other % narrow)
 
 
-def plane_barrier(inner, narrow):
-    barrier = pltpu.get_barrier_semaphore()
-    for offset in range(1, inner * narrow):
-        _, _, device = plane_peer(offset, inner, narrow)
-        pl.semaphore_signal(barrier, inc=1, device_id=device, device_id_type=MESH)
-    pl.semaphore_wait(barrier, inner * narrow - 1)
-
-
-def tile_kernel(inner, narrow, tile_ref, out_ref, send_sem, recv_sem):
-    plane_barrier(inner, narrow)
-    copies = []
-    for offset in range(1, inner * narrow):
-        mine, _, device = plane_peer(offset, inner, narrow)
-        copy = pltpu.make_async_remote_copy(
-            src_ref=tile_ref,
-            dst_ref=out_ref.at[mine],
-            send_sem=send_sem.at[offset - 1],
-            recv_sem=recv_sem.at[offset - 1],
-            device_id=device,
-            device_id_type=MESH,
-        )
-        copy.start()
-        copies.append(copy)
-    mine, _, _ = plane_peer(0, inner, narrow)
-    out_ref[mine] = tile_ref[...]
-    for copy in copies:
-        copy.wait()
-
-
-def share_tile(tile, inner, narrow):
-    group = inner * narrow
-    return pl.pallas_call(
-        functools.partial(tile_kernel, inner, narrow),
-        out_shape=jax.ShapeDtypeStruct((group,) + tile.shape, tile.dtype),
-        in_specs=[pl.BlockSpec(memory_space=pltpu.VMEM)],
-        out_specs=pl.BlockSpec(memory_space=pltpu.VMEM),
-        scratch_shapes=[
-            pltpu.SemaphoreType.DMA((group - 1,)),
-            pltpu.SemaphoreType.DMA((group - 1,)),
-        ],
-        compiler_params=pltpu.CompilerParams(collective_id=0, has_side_effects=True),
-        name="share_tile",
-    )(tile)
-
-
-def total_kernel(devices, narrow, tile_ref, out_ref, held, send_sem, recv_sem):
-    mine = lax.axis_index("wide") * narrow + lax.axis_index("narrow")
-
-    def device_at(offset):
-        other = lax.rem(mine + offset, devices)
-        return (other // narrow, other % narrow)
-
-    barrier = pltpu.get_barrier_semaphore()
-
-    def greet(offset, carry):
-        pl.semaphore_signal(
-            barrier, inc=1, device_id=device_at(offset), device_id_type=MESH
-        )
-        return carry
-
-    def copy_at(offset):
-        return pltpu.make_async_remote_copy(
-            src_ref=tile_ref,
-            dst_ref=held.at[mine],
-            send_sem=send_sem.at[offset - 1],
-            recv_sem=recv_sem.at[offset - 1],
-            device_id=device_at(offset),
-            device_id_type=MESH,
-        )
-
-    def send(offset, carry):
-        copy_at(offset).start()
-        return carry
-
-    def finish(offset, carry):
-        copy_at(offset).wait()
-        return carry
-
-    lax.fori_loop(1, devices, greet, 0)
-    pl.semaphore_wait(barrier, devices - 1)
-    lax.fori_loop(1, devices, send, 0)
-    held[mine] = tile_ref[...]
-    lax.fori_loop(1, devices, finish, 0)
-    out_ref[...] = jnp.sum(held[...], axis=0)
-
-
-def total_over_devices(tile, devices, narrow):
-    return pl.pallas_call(
-        functools.partial(total_kernel, devices, narrow),
-        out_shape=jax.ShapeDtypeStruct(tile.shape, tile.dtype),
-        in_specs=[pl.BlockSpec(memory_space=pltpu.VMEM)],
-        out_specs=pl.BlockSpec(memory_space=pltpu.VMEM),
-        scratch_shapes=[
-            pltpu.VMEM((devices,) + tile.shape, tile.dtype),
-            pltpu.SemaphoreType.DMA((devices - 1,)),
-            pltpu.SemaphoreType.DMA((devices - 1,)),
-        ],
-        compiler_params=pltpu.CompilerParams(collective_id=2, has_side_effects=True),
-        name="total_over_devices",
-    )(tile)
-
-
 def ring_device(shift, inner):
     wide = lax.axis_size("wide")
     return (lax.rem(lax.axis_index("wide") + shift * inner + wide, wide), lax.axis_index("narrow"))
@@ -150,10 +48,61 @@
     pl.semaphore_wait(barrier, group - 1 + (2 if steps > 1 else 0))
 
 
-def gather_kernel(steps, inner, narrow, row_cap, col_cap, rows_ref, cols_ref, dens_ref, *rest):
-    outs, rest = rest[:steps], rest[steps:]
+def any_device(offset):
+    narrow = lax.axis_size("narrow")
+    devices = lax.axis_size("wide") * narrow
+    mine = lax.axis_index("wide") * narrow + lax.axis_index("narrow")
+    other = lax.rem(mine + offset, devices)
+    return mine, (other // narrow, other % narrow)
+
+
+def gather_kernel(
+    steps,
+    inner,
+    narrow,
+    row_cap,
+    col_cap,
+    lists_ref,
+    row_ref,
+    col_ref,
+    counts_ref,
+    tile_ref,
+    weights_ref,
+    dens_ref,
+    orb_ref,
+    harm_ref,
+    tables_ref,
+    rho_ref,
+    total_ref,
+    *rest,
+):
+    arrived, rest = rest[0], rest[1:]
     raws, rest = rest[:steps], rest[steps:]
-    chosen, send_sem, recv_sem, ring_send, ring_recv, own_sem, load_sem = rest
+    (
+        chosen,
+        table,
+        orbs,
+        harms,
+        matrix,
+        moment,
+        share,
+        shares,
+        send_sem,
+        recv_sem,
+        ring_send,
+        ring_recv,
+        own_sem,
+        load_sem,
+        tile_send,
+        tile_recv,
+        local_sem,
+        share_send,
+        share_recv,
+    ) = rest
+    devices = lax.axis_size("wide") * narrow
+    inner_me = lax.axis_index("wide") % inner
+    narrow_me = lax.axis_index("narrow")
+    cap = row_cap * col_cap
     group = inner * narrow
     ring_me = lax.axis_index("wide") // inner
     mine, _, _ = plane_peer(0, inner, narrow)
@@ -186,9 +135,9 @@
         def body(offset, carry):
             _, other, _ = plane_peer(offset, inner, narrow)
             for rr in range(row_cap):
-                row = rows_ref[other, ring * row_cap + rr] * col_blocks
+                row = table[other, 0, (ring * inner + inner_me) * row_cap + rr] * col_blocks
                 for cr in range(col_cap):
-                    place = row + cols_ref[other, cr]
+                    place = row + table[other, 1, narrow_me * col_cap + cr]
                     chosen[step, offset, rr * col_cap + cr] = raws[step][place]
             return carry
 
@@ -198,7 +147,7 @@
         _, _, device = plane_peer(offset, inner, narrow)
         return pltpu.make_async_remote_copy(
             src_ref=chosen.at[step, offset],
-            dst_ref=outs[step].at[mine],
+            dst_ref=arrived.at[pl.ds((step * group + mine) * cap, cap)],
             send_sem=send_sem.at[step, offset - 1],
             recv_sem=recv_sem.at[step, offset - 1],
             device_id=device,
@@ -217,21 +166,74 @@
         )
 
     def own_copy(step):
-        return pltpu.make_async_copy(chosen.at[step, 0], outs[step].at[mine], own_sem.at[step])
-
+        return pltpu.make_async_copy(
+            chosen.at[step, 0],
+            arrived.at[pl.ds((step * group + mine) * cap, cap)],
+            own_sem.at[step],
+        )
+
+    def tile_copy(offset):
+        _, _, device = plane_peer(offset, inner, narrow)
+        return pltpu.make_async_remote_copy(
+            src_ref=tile_ref,
+            dst_ref=tables_ref.at[mine],
+            send_sem=tile_send.at[offset - 1],
+            recv_sem=tile_recv.at[offset - 1],
+            device_id=device,
+            device_id_type=MESH,
+        )
+
+    def share_copy(offset):
+        whose, device = any_device(offset)
+        return pltpu.make_async_remote_copy(
+            src_ref=share,
+            dst_ref=shares.at[whose],
+            send_sem=share_send.at[offset - 1],
+            recv_sem=share_recv.at[offset - 1],
+            device_id=device,
+            device_id_type=MESH,
+        )
+
+    def over(count, make, act):
+        def body(offset, carry):
+            act(make(offset))
+            return carry
+
+        lax.fori_loop(1, count, body, 0)
+
+    start = lambda copy: copy.start()
+    wait = lambda copy: copy.wait()
+
+    load_orbs = pltpu.make_async_copy(orb_ref, orbs, local_sem.at[0])
+    load_harms = pltpu.make_async_copy(harm_ref, harms, local_sem.at[1])
     for step in range(steps):
         if step == 0:
+            tables_ref[mine] = tile_ref[...]
             lax.fori_loop(0, held, load, 0)
+            barrier = pltpu.get_barrier_semaphore()
+
+            def greet(offset, carry):
+                _, device = any_device(offset)
+                pl.semaphore_signal(barrier, inc=1, device_id=device, device_id_type=MESH)
+                return carry
+
+            lax.fori_loop(1, devices, greet, 0)
+            load_orbs.start()
+            load_harms.start()
             lax.fori_loop(0, held, loaded, 0)
-            pick(0)
-            entry_barrier(steps, inner, narrow)
+            pl.semaphore_wait(barrier, devices - 1)
+            over(group, tile_copy, start)
         for piece in range(2):
             if step > 0:
                 ring_copy(step - 1, piece).wait_recv()
             if step < steps - 1:
                 ring_copy(step, piece).start()
-        if step > 0:
-            pick(step)
+        if step == 0:
+            over(group, tile_copy, wait)
+            to_table = pltpu.make_async_copy(tables_ref, table, local_sem.at[2])
+            to_table.start()
+            to_table.wait()
+        pick(step)
 
         def send(offset, carry, step=step):
             block_copy(step, offset).start()
@@ -250,40 +252,104 @@
         if step < steps - 1:
             for piece in range(2):
                 ring_copy(step, piece).wait_send()
-
-
-def gather_blocks(dens, rows, cols, steps, inner, narrow, row_cap, col_cap):
+    load_orbs.wait()
+    load_harms.wait()
+
+    list_len = lists_ref.shape[1]
+    height, points = orbs.shape[1:]
+    each = 2 * BLK
+    moment[...] = jnp.zeros_like(moment)
+
+    def add_batch(batch, carry):
+        places = [lists_ref[batch, k] for k in range(list_len)]
+        cols = [col_ref[place] for place in places]
+        for k in range(list_len):
+            row = row_ref[places[k]]
+            for k2 in range(list_len):
+                spot = row + cols[k2]
+                matrix[k * BLK : (k + 1) * BLK, k2 * BLK : (k2 + 1) * BLK] = arrived[spot]
+        total = jnp.zeros((1, points), jnp.float32)
+        for top in range(0, height, each):
+            product = jnp.dot(
+                matrix[top : top + each, :], orbs[batch], preferred_element_type=jnp.float32
+            )
+            part = product * orbs[batch, top : top + each, :].astype(jnp.float32)
+            total += jnp.sum(part, axis=0, keepdims=True)
+        rho_ref[pl.ds(batch, 1), :] = total
+        live = live_row(weights_ref, counts_ref, batch) * total
+        moment[...] += harms[batch].astype(jnp.float32) * live
+        return carry
+
+    lax.fori_loop(0, orbs.shape[0], add_batch, 0)
+    components = moment.shape[0]
+    diagonal = lax.broadcasted_iota(jnp.int32, (components, LANES), 0) == lax.broadcasted_iota(
+        jnp.int32, (components, LANES), 1
+    )
+    summed = jnp.sum(moment[...], axis=1, keepdims=True)
+    line = jnp.sum(jnp.where(diagonal, summed, 0.0), axis=0, keepdims=True)
+    share[...] = jnp.broadcast_to(line, share.shape)
+    whose, _ = any_device(0)
+    shares[whose] = jnp.broadcast_to(line, share.shape)
+    over(devices, share_copy, start)
+    over(devices, share_copy, wait)
+    line = jnp.sum(shares[...], axis=0)[0:1]
+    total_ref[...] = jnp.sum(jnp.where(diagonal, line, 0.0), axis=1, keepdims=True)
+
+
+def gather_density(
+    lists, rows, cols, counts, tile, weights, dens, orbitals, harmonics, steps, inner, narrow, caps
+):
+    row_cap, col_cap = caps
     group = inner * narrow
     cap = row_cap * col_cap
+    devices = steps * group
     ring_sems = max(1, steps - 1)
     held = dens.shape[0] // BLK * (dens.shape[1] // BLK)
+    batches, height, points = orbitals.shape
+    components = harmonics.shape[1]
+    vmem = pl.BlockSpec(memory_space=pltpu.VMEM)
+    smem = pl.BlockSpec(memory_space=pltpu.SMEM)
+    anywhere = pl.BlockSpec(memory_space=pl.ANY)
     return pl.pallas_call(
         functools.partial(gather_kernel, steps, inner, narrow, row_cap, col_cap),
-        out_shape=[jax.ShapeDtypeStruct((group, cap, BLK, BLK), dens.dtype)] * steps,
-        in_specs=[
-            pl.BlockSpec(memory_space=pltpu.SMEM),
-            pl.BlockSpec(memory_space=pltpu.SMEM),
-            pl.BlockSpec(memory_space=pl.ANY),
+        out_shape=[
+            jax.ShapeDtypeStruct((group,) + tile.shape, tile.dtype),
+            jax.ShapeDtypeStruct((batches, points), jnp.float32),
+            jax.ShapeDtypeStruct((components, 1), jnp.float32),
         ],
-        out_specs=[pl.BlockSpec(memory_space=pl.ANY)] * steps,
-        scratch_shapes=[pltpu.VMEM((held, BLK, BLK), dens.dtype)] * steps
+        in_specs=[smem] * 4 + [vmem] * 2 + [anywhere] * 3,
+        out_specs=[vmem] * 3,
+        scratch_shapes=[pltpu.VMEM((steps * group * cap, BLK, BLK), dens.dtype)]
+        + [pltpu.VMEM((held, BLK, BLK), dens.dtype)] * steps
         + [
             pltpu.VMEM((steps, group, cap, BLK, BLK), dens.dtype),
+            pltpu.SMEM((group,) + tile.shape, tile.dtype),
+            pltpu.VMEM(orbitals.shape, orbitals.dtype),
+            pltpu.VMEM(harmonics.shape, harmonics.dtype),
+            pltpu.VMEM((height, height), dens.dtype),
+            pltpu.VMEM((components, points), jnp.float32),
+            pltpu.VMEM((8, LANES), jnp.float32),
+            pltpu.VMEM((devices, 8, LANES), jnp.float32),
             pltpu.SemaphoreType.DMA((steps, group - 1)),
             pltpu.SemaphoreType.DMA((steps, group - 1)),
             pltpu.SemaphoreType.DMA((ring_sems, 2)),
             pltpu.SemaphoreType.DMA((ring_sems, 2)),
             pltpu.SemaphoreType.DMA((steps,)),
             pltpu.SemaphoreType.DMA((held,)),
+            pltpu.SemaphoreType.DMA((group - 1,)),
+            pltpu.SemaphoreType.DMA((group - 1,)),
+            pltpu.SemaphoreType.DMA((3,)),
+            pltpu.SemaphoreType.DMA((devices - 1,)),
+            pltpu.SemaphoreType.DMA((devices - 1,)),
         ],
         compiler_params=pltpu.CompilerParams(
-            collective_id=1, has_side_effects=True, vmem_limit_bytes=VMEM_BYTES
+            collective_id=1, has_side_effects=True, vmem_limit_bytes=63 * 1024 * 1024
         ),
-        name="gather_blocks",
-    )(rows, cols, dens)
-
-
-def return_kernel(steps, inner, narrow, cap, rows_ref, cols_ref, *rest):
+        name="gather_density",
+    )(lists, rows, cols, counts, tile, weights, dens, orbitals, harmonics)
+
+
+def return_kernel(steps, inner, narrow, cap, table_ref, *rest):
     parts, rest = rest[:steps], rest[steps:]
     out_ref, rest = rest[0], rest[1:]
     gots, rest = rest[:steps], rest[steps:]
@@ -296,6 +362,8 @@
     row_blocks = out_ref.shape[0] // BLK
     col_blocks = out_ref.shape[1] // BLK
     empty = group * cap
+    inner_me = lax.axis_index("wide") % inner
+    narrow_me = lax.axis_index("narrow")
 
     def block_copy(step, offset):
         _, other, device = plane_peer(offset, inner, narrow)
@@ -355,7 +423,7 @@
                 ring_copy(step - 1, piece).wait_recv()
             span = pl.ds(pl.multiple_of(piece * BLK, BLK), BLK)
             bases = [
-                rows_ref[source, ring * row_blocks + piece] + source * cap
+                table_ref[source, 2, (ring * inner + inner_me) * row_blocks + piece] + source * cap
                 for source in range(group)
             ]
 
@@ -366,7 +434,8 @@
                 else:
                     total = jnp.zeros((BLK, BLK), jnp.float32)
                 for source in range(group):
-                    place = jnp.minimum(bases[source] + cols_ref[source, block], empty)
+                    col = table_ref[source, 3, narrow_me * col_blocks + block]
+                    place = jnp.minimum(bases[source] + col, empty)
                     total += gots[step][place].astype(jnp.float32)
                 if last:
                     out_ref[span, across] = total
@@ -402,7 +471,7 @@
             lax.fori_loop(0, row_blocks, left, 0)
 
 
-def return_blocks(parts, rows, cols, shape, steps, inner, narrow, cap):
+def return_blocks(parts, tables, shape, steps, inner, narrow, cap):
     group = inner * narrow
     ring_sems = max(1, steps - 1)
     row_blocks = shape[0] // BLK
@@ -410,7 +479,7 @@
     return pl.pallas_call(
         functools.partial(return_kernel, steps, inner, narrow, cap),
         out_shape=jax.ShapeDtypeStruct(shape, jnp.float32),
-        in_specs=[pl.BlockSpec(memory_space=pltpu.SMEM)] * 2
+        in_specs=[pl.BlockSpec(memory_space=pltpu.SMEM)]
         + [pl.BlockSpec(memory_space=pl.ANY)] * steps,
         out_specs=pl.BlockSpec(memory_space=pltpu.VMEM),
         scratch_shapes=[pltpu.VMEM((group * cap + 1, BLK, BLK), dtype)] * steps
@@ -426,7 +495,7 @@
             collective_id=3, has_side_effects=True, vmem_limit_bytes=VMEM_BYTES
         ),
         name="return_blocks",
-    )(rows, cols, *parts)
+    )(tables, *parts)
 
 
 def live_row(weights_ref, counts_ref, batch):
@@ -435,83 +504,6 @@
     return jnp.where(
         point < counts_ref[batch], weights_ref[pl.ds(batch, 1), :], jnp.float32(0.0)
     )
-
-
-def density_kernel(
-    steps, list_len, lists_ref, row_ref, col_ref, counts_ref, orb_ref, harm_ref, weights_ref, *rest
-):
-    chunks = rest[:steps]
-    rho_ref, moment_ref, held, matrix, sems = rest[steps:]
-    batch = pl.program_id(0)
-    per_chunk = held.shape[0] // steps
-
-    @pl.when(batch == 0)
-    def _():
-        copies = [
-            pltpu.make_async_copy(
-                chunks[k], held.at[pl.ds(k * per_chunk, per_chunk)], sems.at[k]
-            )
-            for k in range(steps)
-        ]
-        for copy in copies:
-            copy.start()
-        moment_ref[...] = jnp.zeros_like(moment_ref)
-        for copy in copies:
-            copy.wait()
-
-    places = [lists_ref[batch, k] for k in range(list_len)]
-    cols = [col_ref[place] for place in places]
-    for k in range(list_len):
-        row = row_ref[places[k]]
-        for k2 in range(list_len):
-            matrix[k * BLK : (k + 1) * BLK, k2 * BLK : (k2 + 1) * BLK] = held[row + cols[k2]]
-    orbs = orb_ref[0]
-    rows_each = 2 * BLK
-    total = jnp.zeros((1, orbs.shape[1]), jnp.float32)
-    for top in range(0, list_len * BLK, rows_each):
-        product = jnp.dot(
-            matrix[top : top + rows_each, :], orbs, preferred_element_type=jnp.float32
-        )
-        part = product * orb_ref[0, top : top + rows_each, :].astype(jnp.float32)
-        total += jnp.sum(part, axis=0, keepdims=True)
-    rho_ref[pl.ds(batch, 1), :] = total
-    live = live_row(weights_ref, counts_ref, batch) * total
-    moment_ref[...] += harm_ref[0].astype(jnp.float32) * live
-
-
-def density_points(lists, rows, cols, counts, orbitals, harmonics, weights, chunks):
-    batches, height, points = orbitals.shape
-    list_len = lists.shape[1]
-    components = harmonics.shape[1]
-    steps = len(chunks)
-    blocks = [chunk.reshape(-1, BLK, BLK) for chunk in chunks]
-    held = steps * blocks[0].shape[0]
-    full = lambda shape: pl.BlockSpec(shape, lambda g, *_: (0, 0))
-    return pl.pallas_call(
-        functools.partial(density_kernel, steps, list_len),
-        out_shape=[
-            jax.ShapeDtypeStruct((batches, points), jnp.float32),
-            jax.ShapeDtypeStruct((components, points), jnp.float32),
-        ],
-        grid_spec=pltpu.PrefetchScalarGridSpec(
-            num_scalar_prefetch=4,
-            grid=(batches,),
-            in_specs=[
-                pl.BlockSpec((1, height, points), lambda g, *_: (g, 0, 0)),
-                pl.BlockSpec((1, components, points), lambda g, *_: (g, 0, 0)),
-                full((batches, points)),
-            ]
-            + [pl.BlockSpec(memory_space=pl.ANY)] * steps,
-            out_specs=[full((batches, points)), full((components, points))],
-            scratch_shapes=[
-                pltpu.VMEM((held, BLK, BLK), jnp.bfloat16),
-                pltpu.VMEM((height, height), jnp.bfloat16),
-                pltpu.SemaphoreType.DMA((steps,)),
-            ],
-        ),
-        compiler_params=pltpu.CompilerParams(vmem_limit_bytes=VMEM_BYTES),
-        name="density_points",
-    )(lists, rows, cols, counts, orbitals, harmonics, weights, *blocks)
 
 
 def integral_kernel(
@@ -637,9 +629,7 @@
     col_cap = region // narrow
     cap = row_cap * col_cap
     wide_me = lax.axis_index("wide")
-    narrow_me = lax.axis_index("narrow")
     ring_me = wide_me // inner
-    inner_me = wide_me % inner
 
     known = block_slot.shape[0]
     hit = region_blocks[:, None] == jnp.arange(known)[None, :]
@@ -657,41 +647,28 @@
     )
     col_back = far + spread(col_owner * col_blocks + col_local, col_rank - far, LANES)
     tile = jnp.stack([row_table, col_table, row_back, col_back] * 2)
-    tables = share_tile(tile, inner, narrow)
-
-    def rows_here(plane, each):
-        used = tables[:, plane, : wide * each].reshape(group, steps, inner, each)
-        one = lax.dynamic_index_in_dim(used, inner_me, axis=2, keepdims=False)
-        return one.reshape(group, steps * each)
-
-    def cols_here(plane, each):
-        return lax.dynamic_slice_in_dim(tables[:, plane], narrow_me * each, each, axis=1)
-
-    chunks = gather_blocks(
-        density,
-        rows_here(0, row_cap),
-        cols_here(1, col_cap),
-        steps,
-        inner,
-        narrow,
-        row_cap,
-        col_cap,
-    )
-
     col_place = col_owner * cap + col_rank
     in_plane = row_owner % inner * (narrow * cap) + row_rank * col_cap
     owner_ring = row_owner // inner
     row_in = (ring_me - owner_ring + steps) % steps * (group * cap) + in_plane
     row_out = (ring_me - 1 - owner_ring + 2 * steps) % steps * (group * cap) + in_plane
 
-    rho, moment_parts = density_points(
-        basis_lists, row_in, col_place, point_counts, orbitals, harmonics, weights, chunks
+    tables, rho, moments = gather_density(
+        basis_lists,
+        row_in,
+        col_place,
+        point_counts,
+        tile,
+        weights,
+        density,
+        orbitals,
+        harmonics,
+        steps,
+        inner,
+        narrow,
+        (row_cap, col_cap),
     )
     components = harmonics.shape[1]
-    local = jnp.sum(moment_parts, axis=1)
-    tile = jnp.zeros((8, LANES), jnp.float32).at[0, :components].set(local)
-    moments = total_over_devices(tile, devices, narrow)[0, :components].reshape(components, 1)
-
     total_points = orbitals.shape[0] * orbitals.shape[2] * devices
     parts = integrals(
         basis_lists,
@@ -709,8 +686,7 @@
     )
     return return_blocks(
         parts,
-        rows_here(2, row_blocks),
-        cols_here(3, col_blocks),
+        tables,
         density.shape,
         steps,
         inner,

time: 271 us -> 248 us (0.915)
  Pallas kernels: 251 us -> 237 us
  local copies, waits for them, and re-layouts: 12.3 us -> 5.13 us
    pallas_call x4 -> x1, Pallas kernels: 135 us -> 120 us  [gather_density(): pl.pallas_call(functools.partial(gather_kernel, steps, inner, narrow, row...]
where the time goes in v3:
time: 248 us; the launch traced here: 245 us
  Pallas kernels  237 us (96%)
  local copies, waits for them, and re-layouts  5.13 us (2%)
  other arithmetic  3.12 us (1%)
    pallas_call x1, Pallas kernels, gather_density(): pl.pallas_call(functools.partial(gather_kernel, steps, inner, narrow, row...  120 us
    pallas_call x1, Pallas kernels, return_blocks(): pl.pallas_call(functools.partial(return_kernel, steps, inner, narrow, cap...  97 us
    pallas_call x1, Pallas kernels, integrals(): pl.pallas_call(functools.partial(integral_kernel, steps, list_len, far_sc...  19.6 us

profile of v3, /device:TPU:0, one launch (start us, length us, event | category | flops | bytes accessed | tf_op | source)
XLA Modules:
  0.0 245.0 jit_solution(2188989772643438343)
XLA Ops:
  0.0 0.9 select_reduce_fusion.4
  0.9 0.2 convert_reduce_fusion
  1.1 0.2 convert_reduce_fusion.1
  1.2 0.6 multiply_add_fusion.1
  1.8 0.5 fusion.7
  2.4 0.1 select_reduce_fusion
  2.5 0.1 select_reduce_fusion.2
  2.5 0.6 fusion.3.row_ref
  3.1 0.6 stack.8.tile_ref
  3.8 1.4 copy.11.lists_ref
  5.1 120.2 %gather_density.1 = (s32[8,8,128]{2,1,0:T(8,128)}, f32[12,256]{1,0:T(8,128)}, f32[64,1]{1,0:T(8,128)}) custom-call(s32[12,8]{1,0:T(8,128)} %copy.11.lists_ref, s32[16]{0:T(128)} %fusion.3.row_ref, s32[16]{0:T(128)} %get-tuple-element.29.col_ref, s32[12]{0:T(128)} %counts_ref.3, s32[8,128]{1,0:T(8,128)} %stack.8.tile_ref, f32[12,256]{1,0:T(8,128)} %weights_ref.3, ...), custom_call_target="tpu_custom_call" | custom-call | tf_op jit(solution)/shard_map/gather_density/pallas_call | solution.py:313
  125.3 19.6 %integrals.1 = (bf16[64,128,128]{2,1,0:T(8,128)(2,1)}, bf16[64,128,128]{2,1,0:T(8,128)(2,1)}, bf16[64,128,128]{2,1,0:T(8,128)(2,1)}, bf16[64,128,128]{2,1,0:T(8,128)(2,1)}) custom-call(s32[12,8]{1,0:T(8,128)} %copy.11.lists_ref, s32[16]{0:T(128)} %get-tuple-element.19.row_ref, s32[16]{0:T(128)} %get-tuple-element.29.col_ref, s32[12]{0:T(128)} %counts_ref.3, ...), custom_call_target="tpu_custom_call" | custom-call | tf_op jit(solution)/shard_map/integrals/pallas_call | solution.py:582
  144.9 97.0 %return_blocks.1 = f32[512,1024]{1,0:T(8,128)} custom-call(s32[8,8,128]{2,1,0:T(8,128)} %get-tuple-element.12.table_ref, bf16[64,128,128]{2,1,0:T(8,128)(2,1)} %get-tuple-element.15.rest_0_, bf16[64,128,128]{2,1,0:T(8,128)(2,1)} %get-tuple-element.16.rest_1_, bf16[64,128,128]{2,1,0:T(8,128)(2,1)} %get-tuple-element.17.rest_2_, ...), custom_call_target="tpu_custom_call" | custom-call | tf_op jit(solution)/shard_map/return_blocks/pallas_call | solution.py:479
  241.9 3.2 %copy.14 = f32[512,1024]{1,0:T(8,128)} copy(f32[512,1024]{1,0:T(8,128)} %return_blocks.1) | data formatting | bytes 4194304
  (3 shorter events, 0.0 us)
